TPU v7x, 32 devices: a whole 2x2x4 slice. The times are simulated.
32 devices in a mesh: ctx: 8 (over z, x), heads: 4 (over y, core).
Axes of the slice: x: 2, y: 2, z: 4, core: 2. Of those that a mesh axis runs over, the one named last changes fastest.
Arguments:
- activations: bfloat16 [2048, 8192], P('ctx', 'heads'), may hold values from -20 to 20
- w_query: bfloat16 [8192, 4096], P(None, 'heads'), may hold values from -0.0625 to 0.0625
- w_key: bfloat16 [8192, 1024], P(None, 'heads'), may hold values from -0.0625 to 0.0625
- w_value: bfloat16 [8192, 1024], P(None, 'heads'), may hold values from -0.0625 to 0.0625
- doc_lengths: int32 [8], replicated, may hold values from 1 to 1024, 2048 in all
- block_dest: int32 [32], replicated, may hold values from 0 to 7, as said below
- out_grad: bfloat16 [2048, 4096], P('ctx', 'heads'), may hold values from -6 to 6
Outputs:
- attention: bfloat16 [2048, 4096], P('ctx', 'heads')
- input_grad: bfloat16 [2048, 8192], P('ctx', 'heads')
Inputs may be any that keep to these rules, and one draw needn't show every extreme that they name: `block_dest`: loader block b lies on loader shard b // 4. Each loader shard sends its blocks to different context shards, and each context shard receives exactly 4 blocks, from different loader shards.
All inputs are finite; a program needn't handle non-finite values.
Results may differ from a plain program's by a relative error of at most 0.025.
The roundings to bfloat16 on the way count: a program that leaves them out, or rounds other values in their place, can miss the bound.
Values may be sent and summed in bfloat16 or wider, within the bound.
A program may use at most 128 MiB of HBM per device.

v0:
```python
import math

import jax
import jax.numpy as jnp
from jax import lax
from jax.sharding import PartitionSpec as P

HD = 128
QPK = 4


NEG = -1e30


def from_behind(value, axis, steps):
    count = lax.axis_size(axis)
    pairs = [(source, (source + steps) % count) for source in range(count)]
    return lax.ppermute(value, axis, pairs)


def layout(block_dest, block_rows):
    nblk = block_dest.shape[0]
    index = jnp.arange(nblk, dtype=jnp.int32)
    order_key = block_dest * nblk + index
    ranks = jnp.sum((order_key[None, :] < order_key[:, None]).astype(jnp.int32), axis=1)
    ctx_blocks = jnp.sum(jnp.where(ranks[None, :] == index[:, None], index[None, :], 0), axis=1)
    ctx_pos = (
        ctx_blocks[:, None] * block_rows + jnp.arange(block_rows, dtype=jnp.int32)[None, :]
    ).reshape(-1)
    return (ctx_blocks, ctx_pos)


def doc_ids(positions, doc_lengths):
    ends = jnp.cumsum(doc_lengths)
    return jnp.sum((ends[None, :] <= positions[:, None]).astype(jnp.int32), axis=1)


def spread(table, array, block_rows):
    width = array.shape[-1]
    grouped = array.reshape(table.shape[1], block_rows, width)
    moved = jnp.einsum("ab,brf->arf", table, grouped, preferred_element_type=jnp.float32)
    return moved.astype(jnp.bfloat16)


def transposed_dot(left, weight):
    return lax.dot_general(
        left, weight, (((1,), (1,)), ((), ())), preferred_element_type=jnp.float32
    )


def per_device(activations, w_query, w_key, w_value, doc_lengths, block_dest, out_grad):
    ctx_count = lax.axis_size("ctx")
    ctx_rank = lax.axis_index("ctx")
    tok_dev = activations.shape[0]
    block_rows = tok_dev * ctx_count // block_dest.shape[0]
    blocks_here = tok_dev // block_rows
    head_dim = HD
    groups = w_key.shape[1] // head_dim
    per_group = QPK
    scale = 1.0 / math.sqrt(head_dim)
    ctx_blocks, ctx_pos = layout(block_dest, block_rows)
    ctx_doc = doc_ids(ctx_pos, doc_lengths)
    my_pos = lax.dynamic_slice_in_dim(ctx_pos, ctx_rank * tok_dev, tok_dev, 0)
    my_doc = lax.dynamic_slice_in_dim(ctx_doc, ctx_rank * tok_dev, tok_dev, 0)
    piece = lax.all_gather(activations, "heads", axis=1, tiled=True)
    rows = piece.shape[1]
    proj_q = jnp.dot(piece, w_query, preferred_element_type=jnp.float32)
    proj_k = jnp.dot(piece, w_key, preferred_element_type=jnp.float32)
    proj_v = jnp.dot(piece, w_value, preferred_element_type=jnp.float32)
    loader_q = proj_q.astype(jnp.bfloat16)
    loader_k = proj_k.astype(jnp.bfloat16)
    loader_v = proj_v.astype(jnp.bfloat16)
    slots = jnp.arange(ctx_count, dtype=jnp.int32)
    my_dest = lax.dynamic_slice_in_dim(block_dest, ctx_rank * blocks_here, blocks_here, 0)
    send_map = (my_dest[None, :] == slots[:, None]).astype(jnp.bfloat16)
    mine = lax.dynamic_slice_in_dim(ctx_blocks, ctx_rank * blocks_here, blocks_here, 0)
    source = mine // blocks_here
    take_map = (source[:, None] == slots[None, :]).astype(jnp.bfloat16)
    recv_q, recv_k, recv_v = (
        lax.all_to_all(
            spread(send_map, loader_q, block_rows), "ctx", split_axis=0, concat_axis=0, tiled=True
        ),
        lax.all_to_all(
            spread(send_map, loader_k, block_rows), "ctx", split_axis=0, concat_axis=0, tiled=True
        ),
        lax.all_to_all(
            spread(send_map, loader_v, block_rows), "ctx", split_axis=0, concat_axis=0, tiled=True
        ),
    )
    ctx_q = spread(take_map, recv_q.reshape(ctx_count * block_rows, -1), block_rows).reshape(
        tok_dev, -1
    )
    ctx_k = spread(take_map, recv_k.reshape(ctx_count * block_rows, -1), block_rows).reshape(
        tok_dev, -1
    )
    ctx_v = spread(take_map, recv_v.reshape(ctx_count * block_rows, -1), block_rows).reshape(
        tok_dev, -1
    )
    query_four = ctx_q.reshape(tok_dev, groups, per_group, head_dim)

    def visible(key_pos, key_doc):
        return (my_doc[:, None] == key_doc[None, :]) & (key_pos[None, :] <= my_pos[:, None])

    def attend(state, key_blk, value_blk, key_pos, key_doc):
        mask = visible(key_pos, key_doc)

        def attend_run(inner):
            m_old, l_old, accum = inner
            scores = (
                jnp.einsum(
                    "tgqe,sge->gqts", query_four, key_blk, preferred_element_type=jnp.float32
                )
                * scale
            )
            scores = jnp.where(mask[None, None], scores, NEG)
            m_new = jnp.maximum(m_old, jnp.max(scores, axis=-1))
            factor = jnp.exp(m_old - m_new)
            probs = jnp.where(mask[None, None], jnp.exp(scores - m_new[..., None]), 0.0)
            l_new = l_old * factor + jnp.sum(probs, axis=-1)
            accum = accum * factor[..., None] + jnp.einsum(
                "gqts,sge->gqte",
                probs,
                value_blk.astype(jnp.float32),
                precision=lax.Precision.HIGHEST,
                preferred_element_type=jnp.float32,
            )
            return (m_new, l_new, accum)

        return lax.cond(jnp.any(mask), attend_run, lambda inner: inner, state)

    start_state = (
        jnp.full((groups, per_group, tok_dev), NEG, jnp.float32),
        jnp.zeros((groups, per_group, tok_dev), jnp.float32),
        jnp.zeros((groups, per_group, tok_dev, head_dim), jnp.float32),
    )
    grad_four = out_grad.reshape(tok_dev, groups, per_group, head_dim)

    def grads_over(dquery, key_piece, value_piece, start, lse, delta):
        rows = key_piece.shape[0]
        width = math.gcd(rows, 512)

        def grads_one_block(index, inner):
            dq_sum, dk_rows, dv_rows = inner
            offset = index * width
            key_blk = key_piece.reshape(width, groups, head_dim)
            value_blk = value_piece.reshape(width, groups, head_dim)
            key_pos = lax.dynamic_slice_in_dim(ctx_pos, start + offset, width, 0)
            key_doc = lax.dynamic_slice_in_dim(ctx_doc, start + offset, width, 0)
            mask = visible(key_pos, key_doc)

            def one_run(unused):
                scores = (
                    jnp.einsum(
                        "tgqe,sge->gqts", query_four, key_blk, preferred_element_type=jnp.float32
                    )
                    * scale
                )
                weights = jnp.where(mask[None, None], jnp.exp(scores - lse[..., None]), 0.0)
                weights_b = weights.astype(jnp.bfloat16)
                dv_blk = jnp.einsum(
                    "gqts,tgqe->sge", weights_b, grad_four, preferred_element_type=jnp.float32
                )
                dprob = jnp.einsum(
                    "tgqe,sge->gqts", grad_four, value_blk, preferred_element_type=jnp.float32
                )
                dscore = (weights * (dprob - delta[..., None]) * scale).astype(jnp.bfloat16)
                dq_add = jnp.einsum(
                    "gqts,sge->tgqe", dscore, key_blk, preferred_element_type=jnp.float32
                )
                dk_blk = jnp.einsum(
                    "gqts,tgqe->sge", dscore, query_four, preferred_element_type=jnp.float32
                )
                return (dq_add, dk_blk, dv_blk)

            def skip(unused):
                return (
                    jnp.zeros((tok_dev, groups, per_group, head_dim), jnp.float32),
                    jnp.zeros((width, groups, head_dim), jnp.float32),
                    jnp.zeros((width, groups, head_dim), jnp.float32),
                )

            dq_add, dk_blk, dv_blk = lax.cond(jnp.any(mask), one_run, skip, 0)
            dk_rows = dk_blk.reshape(width, groups * head_dim)
            dv_rows = dv_blk.reshape(width, groups * head_dim)
            return (dq_sum + dq_add, dk_rows, dv_rows)

        empty_rows = jnp.zeros((rows, groups * head_dim), jnp.float32)
        return lax.fori_loop(0, rows // width, grads_one_block, (dquery, empty_rows, empty_rows))

    dq_start = jnp.zeros((tok_dev, groups, per_group, head_dim), jnp.float32)
    key_piece = lax.all_gather(ctx_k, "ctx", axis=0, tiled=True)
    value_piece = lax.all_gather(ctx_v, "ctx", axis=0, tiled=True)
    rows = key_piece.shape[0]
    width = math.gcd(rows, 512)

    def fold_one_block(index, inner):
        offset = index * width
        key_blk = lax.dynamic_slice_in_dim(key_piece, offset, width, 0).reshape(
            width, groups, head_dim
        )
        value_blk = lax.dynamic_slice_in_dim(value_piece, offset, width, 0).reshape(
            width, groups, head_dim
        )
        key_pos = lax.dynamic_slice_in_dim(ctx_pos, offset, width, 0)
        key_doc = lax.dynamic_slice_in_dim(ctx_doc, offset, width, 0)
        return attend(inner, key_blk, value_blk, key_pos, key_doc)

    m_end, l_end, accum = lax.fori_loop(0, rows // width, fold_one_block, start_state)
    attn = (accum / l_end[..., None]).astype(jnp.bfloat16)
    attention = attn.transpose(2, 0, 1, 3).reshape(tok_dev, groups * per_group * head_dim)
    lse = m_end + jnp.log(l_end)
    attn_four = attention.reshape(tok_dev, groups, per_group, head_dim)
    delta = jnp.einsum(
        "tgqe,tgqe->gqt", grad_four.astype(jnp.float32), attn_four.astype(jnp.float32)
    )

    def turn(step, inner):
        dquery, key_now, value_now, dk_now, dv_now = inner
        owner = jnp.mod(ctx_rank - step, ctx_count)
        dquery, dk_add, dv_add = grads_over(dquery, key_now, value_now, owner * tok_dev, lse, delta)
        dk_now, dv_now = (
            from_behind((dk_now + dk_add).astype(jnp.bfloat16), "ctx", 1).astype(jnp.float32),
            from_behind((dv_now + dv_add).astype(jnp.bfloat16), "ctx", 1).astype(jnp.float32),
        )
        key_now, value_now = from_behind((key_now, value_now), "ctx", 1)
        return (dquery, key_now, value_now, dk_now, dv_now)

    zero_grads = jnp.zeros((tok_dev, groups * head_dim), jnp.float32)
    dquery, unused_k, unused_v, dkey, dvalue = lax.fori_loop(
        0, ctx_count, turn, (dq_start, ctx_k, ctx_v, zero_grads, zero_grads)
    )
    dq_ctx = dquery.reshape(tok_dev, groups * per_group * head_dim).astype(jnp.bfloat16)
    dk_ctx = dkey.astype(jnp.bfloat16)
    dv_ctx = dvalue.astype(jnp.bfloat16)
    back_map = take_map.T
    home_q, home_k, home_v = (
        lax.all_to_all(
            spread(back_map, dq_ctx, block_rows), "ctx", split_axis=0, concat_axis=0, tiled=True
        ),
        lax.all_to_all(
            spread(back_map, dk_ctx, block_rows), "ctx", split_axis=0, concat_axis=0, tiled=True
        ),
        lax.all_to_all(
            spread(back_map, dv_ctx, block_rows), "ctx", split_axis=0, concat_axis=0, tiled=True
        ),
    )
    pick_map = send_map.T
    dq_loader = spread(pick_map, home_q.reshape(ctx_count * block_rows, -1), block_rows).reshape(
        tok_dev, -1
    )
    dk_loader = spread(pick_map, home_k.reshape(ctx_count * block_rows, -1), block_rows).reshape(
        tok_dev, -1
    )
    dv_loader = spread(pick_map, home_v.reshape(ctx_count * block_rows, -1), block_rows).reshape(
        tok_dev, -1
    )
    grad_terms = (
        transposed_dot(dq_loader, w_query)
        + transposed_dot(dk_loader, w_key)
        + transposed_dot(dv_loader, w_value)
    )
    input_grad = lax.psum_scatter(
        grad_terms.astype(jnp.bfloat16), "heads", scatter_dimension=1, tiled=True
    )
    return (attention, input_grad)


def solution(mesh):
    return jax.shard_map(
        per_device,
        mesh=mesh,
        in_specs=(
            P("ctx", "heads"),
            P(None, "heads"),
            P(None, "heads"),
            P(None, "heads"),
            P(),
            P(),
            P("ctx", "heads"),
        ),
        out_specs=(P("ctx", "heads"), P("ctx", "heads")),
        check_vma=False,
    )
```

profile of v0, /device:TPU:16, one launch (start us, length us, event | category | flops | bytes accessed | tf_op | source)
XLA Modules:
  0.0 551.2 jit_solution(3324979120740839685)
XLA Ops:
  9.7 35.5 %all-gather.4.cloned.1.call-done = bf16[256,8192]{1,0:T(8,128)(2,1)} async-done(((bf16[256,2048]{1,0:T(8,128)(2,1)}), bf16[256,8192]{1,0:T(8,128)(2,1)}) %all-gather.4.cloned.1.call-update) | async-done | bytes 4194320 | tf_op jit(solution)/shard_map/all_gather | solution.py:65
  45.1 4.7 convolution_convert_fusion.13
  51.0 6.0 %all-to-all-start.2 = ((bf16[8,64,256]{2,1,0:T(8,128)(2,1)}), bf16[8,64,256]{2,1,0:T(8,128)(2,1)S(1)}, u32[]{:S(2)}, u32[]{:S(2)}) async-start(bf16[8,64,256]{2,1,0:T(8,128)(2,1)} %copy.111), calls=%async_computation.2 | async-start | bytes 524288 | tf_op jit(solution)/shard_map/all_to_all | solution.py:86
  57.0 4.7 convolution_convert_fusion.14
  64.4 5.5 all-to-all-start
  70.9 11.5 %convolution_convert_fusion.4 = bf16[256,1024]{1,0:T(8,128)(2,1)S(1)} fusion(bf16[256,8192]{1,0:T(8,128)(2,1)} %all-gather.4.cloned.1.call-done, bf16[8192,1024]{1,0:T(8,128)(2,1)} %param.16), kind=kOutput, calls=%fused_computation.45 | convolution fusion | flops 4295229440 | bytes 21495808 | tf_op jit(solution)/shard_map/dot_general | solution.py:67
  84.7 6.0 %all-to-all-start.1 = ((bf16[8,64,1024]{2,1,0:T(8,128)(2,1)}), bf16[8,64,1024]{2,1,0:T(8,128)(2,1)S(1)}, u32[]{:S(2)}, u32[]{:S(2)}) async-start(bf16[8,64,1024]{2,1,0:T(8,128)(2,1)} %copy.107), calls=%async_computation.1 | async-start | bytes 2097152 | tf_op jit(solution)/shard_map/all_to_all | solution.py:80
  96.9 24.2 %all-to-all-done.1 = bf16[8,64,1024]{2,1,0:T(8,128)(2,1)S(1)} async-done(((bf16[8,64,1024]{2,1,0:T(8,128)(2,1)}), bf16[8,64,1024]{2,1,0:T(8,128)(2,1)S(1)}, u32[]{:S(2)}, u32[]{:S(2)}) %all-to-all-start.1) | async-done | bytes 1048608 | tf_op jit(solution)/shard_map/all_to_all | solution.py:80
  125.4 37.9 %all-gather.6.cloned.1.call-done = bf16[2048,256]{1,0:T(8,128)(2,1)} async-done(((bf16[256,256]{1,0:T(8,128)(2,1)}), bf16[2048,256]{1,0:T(8,128)(2,1)}) %all-gather.6.cloned.1.call-update) | async-done | bytes 1048592 | tf_op jit(solution)/shard_map/all_gather | solution.py:191
  163.3 2.3 copy.114
  166.6 47.4 %while.56 = (s32[]{:T(128)}, f32[2,4,256]{2,1,0:T(4,128)S(1)}, f32[2,4,256]{2,1,0:T(4,128)S(1)}, f32[2,4,256,128]{3,2,1,0:T(8,128)}, s32[256]{0:T(256)}, /*index...) while((s32[]{:T(128)}, f32[2,4,256]{2,1,0:T(4,128)S(1)}, ...), condition=%wide.region_10.11_spmd, body=%wide.region_4.10_spmd.sunk | while | flops 1892683776 | bytes 25835900 | solution.py:208
  170.3 8.2 %conditional.5 = ((f32[2,4,256]{2,1,0:T(4,128)S(1)}, f32[2,4,256]{2,1,0:T(4,128)S(1)}, f32[2,4,256,128]{3,2,1,0:T(8,128)})) conditional(s32[]{:T(128)} %convert_element_type.201, (f32[2,4,256]{2,1,0:T(4,128)S(1)}, f32[2,4,256]{2,1,0:T(4,128)S(1)}, f32[2,4,256,128]{3,2,1,0:T(8,128)}) %tuple.116, (pred[256,512]{0,1:T(8,128)(4,1)S(1)}, ...), branch_computations={%region_6.6_spmd, %region_7.9_spmd} | conditional | flops 1892159488 | bytes 25690204 | solution.py:129
  173.3 4.2 fusion.8
  182.1 8.2 %conditional.5 = ((f32[2,4,256]{2,1,0:T(4,128)S(1)}, f32[2,4,256]{2,1,0:T(4,128)S(1)}, f32[2,4,256,128]{3,2,1,0:T(8,128)})) conditional(s32[]{:T(128)} %convert_element_type.201, (f32[2,4,256]{2,1,0:T(4,128)S(1)}, f32[2,4,256]{2,1,0:T(4,128)S(1)}, f32[2,4,256,128]{3,2,1,0:T(8,128)}) %tuple.116, (pred[256,512]{0,1:T(8,128)(4,1)S(1)}, ...), branch_computations={%region_6.6_spmd, %region_7.9_spmd} | conditional | flops 1892159488 | bytes 25690204 | solution.py:129
  185.1 4.2 fusion.8
  194.0 8.2 %conditional.5 = ((f32[2,4,256]{2,1,0:T(4,128)S(1)}, f32[2,4,256]{2,1,0:T(4,128)S(1)}, f32[2,4,256,128]{3,2,1,0:T(8,128)})) conditional(s32[]{:T(128)} %convert_element_type.201, (f32[2,4,256]{2,1,0:T(4,128)S(1)}, f32[2,4,256]{2,1,0:T(4,128)S(1)}, f32[2,4,256,128]{3,2,1,0:T(8,128)}) %tuple.116, (pred[256,512]{0,1:T(8,128)(4,1)S(1)}, ...), branch_computations={%region_6.6_spmd, %region_7.9_spmd} | conditional | flops 1892159488 | bytes 25690204 | solution.py:129
  197.0 4.2 fusion.8
  205.9 8.2 %conditional.5 = ((f32[2,4,256]{2,1,0:T(4,128)S(1)}, f32[2,4,256]{2,1,0:T(4,128)S(1)}, f32[2,4,256,128]{3,2,1,0:T(8,128)})) conditional(s32[]{:T(128)} %convert_element_type.201, (f32[2,4,256]{2,1,0:T(4,128)S(1)}, f32[2,4,256]{2,1,0:T(4,128)S(1)}, f32[2,4,256,128]{3,2,1,0:T(8,128)}) %tuple.116, (pred[256,512]{0,1:T(8,128)(4,1)S(1)}, ...), branch_computations={%region_6.6_spmd, %region_7.9_spmd} | conditional | flops 1892159488 | bytes 25690204 | solution.py:129
  208.9 4.2 fusion.8
  214.1 2.7 fusion.51
  219.1 203.4 %while.57 = (s32[]{:T(128)}, f32[256,2,4,128]{3,0,2,1:T(8,128)S(1)}, bf16[256,256]{1,0:T(8,128)(2,1)}, bf16[256,256]{1,0:T(8,128)(2,1)}, f32[256,256]{0,1:T(8,12...) while((s32[]{:T(128)}, ...), condition=%wide.region_15.16_spmd.clone, body=%wide.region_11.15_spmd.clone.sunk | while | flops 676593664 | bytes 24142468 | solution.py:229
  222.8 2.9 collective-permute-start.1
  229.8 5.6 %conditional.6 = (f32[256,2,4,128]{3,0,2,1:T(8,128)S(1)}, f32[256,256]{0,1:T(8,128)S(1)}, f32[256,256]{0,1:T(8,128)S(1)}) conditional(s32[]{:T(128)} %convert_element_type.204, () %tuple.120, (pred[256,256]{0,1:T(8,128)(4,1)}, bf16[256,256]{1,0:T(8,128)(2,1)}, bf16[256,2,4,128]{0,3,2,1:T(8,128)(2,1)}, f32[2,4,256]{2,1,0:T(4,128)}, ...), branch_computations={%region_13.13_spmd, %region_14.14_spmd} | conditional | flops 675282944 | bytes 16203828 | solution.py:182
  236.1 2.7 collective-permute-start.2
  239.1 2.2 collective-permute-done.3
  247.6 2.3 collective-permute-start.1
  251.5 2.1 fusion.83
  254.1 5.6 %conditional.6 = (f32[256,2,4,128]{3,0,2,1:T(8,128)S(1)}, f32[256,256]{0,1:T(8,128)S(1)}, f32[256,256]{0,1:T(8,128)S(1)}) conditional(s32[]{:T(128)} %convert_element_type.204, () %tuple.120, (pred[256,256]{0,1:T(8,128)(4,1)}, bf16[256,256]{1,0:T(8,128)(2,1)}, bf16[256,2,4,128]{0,3,2,1:T(8,128)(2,1)}, f32[2,4,256]{2,1,0:T(4,128)}, ...), branch_computations={%region_13.13_spmd, %region_14.14_spmd} | conditional | flops 675282944 | bytes 16203828 | solution.py:182
  260.8 4.1 collective-permute-start.2
  269.8 2.4 collective-permute-start
  276.6 2.1 fusion.83
  279.2 5.6 %conditional.6 = (f32[256,2,4,128]{3,0,2,1:T(8,128)S(1)}, f32[256,256]{0,1:T(8,128)S(1)}, f32[256,256]{0,1:T(8,128)S(1)}) conditional(s32[]{:T(128)} %convert_element_type.204, () %tuple.120, (pred[256,256]{0,1:T(8,128)(4,1)}, bf16[256,256]{1,0:T(8,128)(2,1)}, bf16[256,2,4,128]{0,3,2,1:T(8,128)(2,1)}, f32[2,4,256]{2,1,0:T(4,128)}, ...), branch_computations={%region_13.13_spmd, %region_14.14_spmd} | conditional | flops 675282944 | bytes 16203828 | solution.py:182
  286.3 4.5 collective-permute-done.3
  296.0 2.2 collective-permute-start.1
  299.8 2.1 fusion.83
  302.4 5.6 %conditional.6 = (f32[256,2,4,128]{3,0,2,1:T(8,128)S(1)}, f32[256,256]{0,1:T(8,128)S(1)}, f32[256,256]{0,1:T(8,128)S(1)}) conditional(s32[]{:T(128)} %convert_element_type.204, () %tuple.120, (pred[256,256]{0,1:T(8,128)(4,1)}, bf16[256,256]{1,0:T(8,128)(2,1)}, bf16[256,2,4,128]{0,3,2,1:T(8,128)(2,1)}, f32[2,4,256]{2,1,0:T(4,128)}, ...), branch_computations={%region_13.13_spmd, %region_14.14_spmd} | conditional | flops 675282944 | bytes 16203828 | solution.py:182
  310.1 3.6 collective-permute-start.2
  314.1 3.2 collective-permute-done.2
  322.6 2.9 collective-permute-start.1
  327.1 2.1 fusion.83
  329.7 5.6 %conditional.6 = (f32[256,2,4,128]{3,0,2,1:T(8,128)S(1)}, f32[256,256]{0,1:T(8,128)S(1)}, f32[256,256]{0,1:T(8,128)S(1)}) conditional(s32[]{:T(128)} %convert_element_type.204, () %tuple.120, (pred[256,256]{0,1:T(8,128)(4,1)}, bf16[256,256]{1,0:T(8,128)(2,1)}, bf16[256,2,4,128]{0,3,2,1:T(8,128)(2,1)}, f32[2,4,256]{2,1,0:T(4,128)}, ...), branch_computations={%region_13.13_spmd, %region_14.14_spmd} | conditional | flops 675282944 | bytes 16203828 | solution.py:182
  336.4 4.2 collective-permute-start.2
  341.3 2.5 collective-permute-done.2
  349.4 2.5 collective-permute-start.1
  353.5 2.1 fusion.83
  356.1 5.6 %conditional.6 = (f32[256,2,4,128]{3,0,2,1:T(8,128)S(1)}, f32[256,256]{0,1:T(8,128)S(1)}, f32[256,256]{0,1:T(8,128)S(1)}) conditional(s32[]{:T(128)} %convert_element_type.204, () %tuple.120, (pred[256,256]{0,1:T(8,128)(4,1)}, bf16[256,256]{1,0:T(8,128)(2,1)}, bf16[256,2,4,128]{0,3,2,1:T(8,128)(2,1)}, f32[2,4,256]{2,1,0:T(4,128)}, ...), branch_computations={%region_13.13_spmd, %region_14.14_spmd} | conditional | flops 675282944 | bytes 16203828 | solution.py:182
  364.4 4.1 collective-permute-done.3
  373.8 2.4 collective-permute-start.1
  380.3 5.6 %conditional.6 = (f32[256,2,4,128]{3,0,2,1:T(8,128)S(1)}, f32[256,256]{0,1:T(8,128)S(1)}, f32[256,256]{0,1:T(8,128)S(1)}) conditional(s32[]{:T(128)} %convert_element_type.204, () %tuple.120, (pred[256,256]{0,1:T(8,128)(4,1)}, bf16[256,256]{1,0:T(8,128)(2,1)}, bf16[256,2,4,128]{0,3,2,1:T(8,128)(2,1)}, f32[2,4,256]{2,1,0:T(4,128)}, ...), branch_computations={%region_13.13_spmd, %region_14.14_spmd} | conditional | flops 675282944 | bytes 16203828 | solution.py:182
  387.4 4.3 collective-permute-start.2
  396.8 2.2 collective-permute-start
  406.0 5.6 %conditional.6 = (f32[256,2,4,128]{3,0,2,1:T(8,128)S(1)}, f32[256,256]{0,1:T(8,128)S(1)}, f32[256,256]{0,1:T(8,128)S(1)}) conditional(s32[]{:T(128)} %convert_element_type.204, () %tuple.120, (pred[256,256]{0,1:T(8,128)(4,1)}, bf16[256,256]{1,0:T(8,128)(2,1)}, bf16[256,2,4,128]{0,3,2,1:T(8,128)(2,1)}, f32[2,4,256]{2,1,0:T(4,128)}, ...), branch_computations={%region_13.13_spmd, %region_14.14_spmd} | conditional | flops 675282944 | bytes 16203828 | solution.py:182
  412.7 3.1 collective-permute-start.2
  416.1 4.2 collective-permute-done.3
  423.7 4.4 all-to-all-start.5
  430.2 3.7 all-to-all-done.5
  434.0 5.7 %all-to-all-start.4 = ((bf16[8,64,256]{2,1,0:T(8,128)(2,1)}), bf16[8,64,256]{2,1,0:T(8,128)(2,1)S(1)}, u32[]{:S(2)}, u32[]{:S(2)}) async-start(bf16[8,64,256]{2,1,0:T(8,128)(2,1)} %copy.127), calls=%async_computation.4 | async-start | bytes 524288 | tf_op jit(solution)/shard_map/all_to_all | solution.py:240
  442.7 6.8 %all-to-all-done.4 = bf16[8,64,256]{2,1,0:T(8,128)(2,1)S(1)} async-done(((bf16[8,64,256]{2,1,0:T(8,128)(2,1)}), bf16[8,64,256]{2,1,0:T(8,128)(2,1)S(1)}, u32[]{:S(2)}, u32[]{:S(2)}) %all-to-all-start.4) | async-done | bytes 262176 | tf_op jit(solution)/shard_map/all_to_all | solution.py:240
  449.5 6.8 %all-to-all-start.3 = ((bf16[8,64,1024]{2,1,0:T(8,128)(2,1)}), bf16[8,64,1024]{2,1,0:T(8,128)(2,1)S(1)}, u32[]{:S(2)}, u32[]{:S(2)}) async-start(bf16[8,64,1024]{2,1,0:T(8,128)(2,1)} %copy.122), calls=%async_computation.3 | async-start | bytes 2097152 | tf_op jit(solution)/shard_map/all_to_all | solution.py:237
  456.9 12.5 %all-to-all-done.3 = bf16[8,64,1024]{2,1,0:T(8,128)(2,1)S(1)} async-done(((bf16[8,64,1024]{2,1,0:T(8,128)(2,1)}), bf16[8,64,1024]{2,1,0:T(8,128)(2,1)S(1)}, u32[]{:S(2)}, u32[]{:S(2)}) %all-to-all-start.3) | async-done | bytes 1048608 | tf_op jit(solution)/shard_map/all_to_all | solution.py:237
  470.4 18.9 %fusion.56 = f32[256,8192]{1,0:T(8,128)} fusion(bf16[256,1024]{1,0:T(8,128)(2,1)S(1)} %bitcast.128, bf16[8192,1024]{1,0:T(8,128)(2,1)} %param.16), kind=kOutput, calls=%fused_computation.91 | convolution fusion | flops 4294967296 | bytes 25690112 | tf_op jit(solution)/shard_map/dot_general | solution.py:46
  489.3 6.1 %convolution_add_fusion.1 = f32[256,8192]{1,0:T(8,128)S(1)} fusion(f32[256,8192]{1,0:T(8,128)} %fusion.56, bf16[256,256]{1,0:T(8,128)(2,1)S(1)} %bitcast.133, bf16[8192,256]{1,0:T(8,128)(2,1)} %param.17), kind=kOutput, calls=%fused_computation.39 | convolution fusion | flops 1075838976 | bytes 21102592 | tf_op jit(solution)/shard_map/dot_general | solution.py:46
  495.4 3.3 fusion.24
  501.2 43.4 %reduce-scatter.2.cloned.1.call-done = bf16[256,2048]{1,0:T(8,128)(2,1)} async-done(((bf16[256,8192]{1,0:T(8,128)(2,1)}), bf16[256,2048]{1,0:T(8,128)(2,1)}) %reduce-scatter.2.cloned.1.call-update) | async-done | bytes 1048592 | tf_op jit(solution)/shard_map/reduce_scatter | solution.py:262
  (327 shorter events, 186.4 us)
Async XLA Ops:
  7.2 38.0 %all-gather.4.cloned.1.call-start = ((), (), s32[]{:S(2)}) async-start(), calls=%async_computation.7 | async-start | bytes 5242880 | tf_op jit(solution)/shard_map/all_gather | solution.py:65
  8.6 73.8 %copy-start.6 = (s32[4]{0:T(128)}, s32[4]{0:T(128)S(1)}, u32[]{:S(2)}) copy-start(s32[4]{0:T(128)S(1)} %dynamic_slice.75) | copy-start | bytes 52
  9.7 111.5 %copy-start.8 = (s32[4]{0:T(128)}, s32[4]{0:T(128)S(1)}, u32[]{:S(2)}) copy-start(s32[4]{0:T(128)S(1)} %and_select_fusion) | copy-start | bytes 52
  51.0 13.4 %all-to-all-start.2 = ((bf16[8,64,256]{2,1,0:T(8,128)(2,1)}), bf16[8,64,256]{2,1,0:T(8,128)(2,1)S(1)}, u32[]{:S(2)}, u32[]{:S(2)}) async-start(bf16[8,64,256]{2,1,0:T(8,128)(2,1)} %copy.111), calls=%async_computation.2 | async-start | bytes 524288 | tf_op jit(solution)/shard_map/all_to_all | solution.py:86
  64.4 20.3 %all-to-all-start = ((bf16[8,64,256]{2,1,0:T(8,128)(2,1)}), bf16[8,64,256]{2,1,0:T(8,128)(2,1)S(1)}, u32[]{:S(2)}, u32[]{:S(2)}) async-start(bf16[8,64,256]{2,1,0:T(8,128)(2,1)} %copy.103), calls=%async_computation | async-start | bytes 524288 | tf_op jit(solution)/shard_map/all_to_all | solution.py:83
  69.9 53.8 %all-gather.8.cloned.1.call-start = ((), (), s32[]{:S(2)}) async-start(), calls=%async_computation.9 | async-start | bytes 1179648 | tf_op jit(solution)/shard_map/all_gather | solution.py:192
  82.5 9.2 %copy-start.10 = (s32[8]{0:T(128)S(1)}, s32[8]{0:T(128)}, u32[]{:S(2)}) copy-start(s32[8]{0:T(128)} %param.19) | copy-start | bytes 100
  82.5 14.2 %copy-start.5 = (bf16[256,1024]{1,0:T(8,128)(2,1)S(1)}, bf16[256,1024]{1,0:T(8,128)(2,1)}, u32[]{:S(2)}) copy-start(bf16[256,1024]{1,0:T(8,128)(2,1)} %param.21) | copy-start | bytes 1572868
  84.7 36.5 %all-to-all-start.1 = ((bf16[8,64,1024]{2,1,0:T(8,128)(2,1)}), bf16[8,64,1024]{2,1,0:T(8,128)(2,1)S(1)}, u32[]{:S(2)}, u32[]{:S(2)}) async-start(bf16[8,64,1024]{2,1,0:T(8,128)(2,1)} %copy.107), calls=%async_computation.1 | async-start | bytes 2097152 | tf_op jit(solution)/shard_map/all_to_all | solution.py:80
  90.7 72.6 %all-gather.6.cloned.1.call-start = ((), (), s32[]{:S(2)}) async-start(), calls=%async_computation.8 | async-start | bytes 1179648 | tf_op jit(solution)/shard_map/all_gather | solution.py:191
  171.3 2.0 copy-start.1
  177.5 1.0 copy-start.2
  183.2 2.0 copy-start.1
  195.0 2.0 copy-start.1
  201.2 1.0 copy-start.2
  206.9 2.0 copy-start.1
  219.1 203.5 %copy-start.9 = (s32[4]{0:T(128)S(1)}, s32[4]{0:T(128)}, u32[]{:S(2)}) copy-start(s32[4]{0:T(128)} %copy-done.8) | copy-start | bytes 52
  220.6 22.9 %collective-permute-start = (bf16[256,256]{1,0:T(8,128)(2,1)}, bf16[256,256]{1,0:T(8,128)(2,1)}, u32[]{:S(2)}, u32[]{:S(2)}) collective-permute-start(bf16[256,256]{1,0:T(8,128)(2,1)} %copy.227), channel_id=1, source_target_pairs={{0,4},{4,8},{8,12},{12,16},{16,20},{20,24},{24,28},{28,0},{1,5},{5... | collective-permute-start | bytes 393224 | tf_op jit(solution)/shard_map/while/body/eval_jaxpr/ppermute | solution.py:18
  222.8 20.7 %collective-permute-start.1 = (bf16[256,256]{1,0:T(8,128)(2,1)}, bf16[256,256]{1,0:T(8,128)(2,1)}, u32[]{:S(2)}, u32[]{:S(2)}) collective-permute-start(bf16[256,256]{1,0:T(8,128)(2,1)} %copy.228), channel_id=1, source_target_pairs={{0,4},{4,8},{8,12},{12,16},{16,20},{20,24},{24,28},{28,0},{1,5},{5... | collective-permute-start | bytes 393224 | tf_op jit(solution)/shard_map/while/body/eval_jaxpr/ppermute | solution.py:18
  231.7 2.6 copy-start
  235.4 5.9 %collective-permute-start.3 = (bf16[256,256]{0,1:T(8,128)(2,1)S(1)}, bf16[256,256]{0,1:T(8,128)(2,1)S(1)}, u32[]{:S(2)}, u32[]{:S(2)}) collective-permute-start(bf16[256,256]{0,1:T(8,128)(2,1)S(1)} %fusion.85), channel_id=1, source_target_pairs={{0,4},{4,8},{8,12},{12,16},{16,20},{20,24},{24,28},{28,0},{1,5},{5... | collective-permute-start | bytes 393224 | tf_op jit(solution)/shard_map/while/body/eval_jaxpr/ppermute | solution.py:18
  236.1 6.7 %collective-permute-start.2 = (bf16[256,256]{0,1:T(8,128)(2,1)S(1)}, bf16[256,256]{0,1:T(8,128)(2,1)S(1)}, u32[]{:S(2)}, u32[]{:S(2)}) collective-permute-start(bf16[256,256]{0,1:T(8,128)(2,1)S(1)} %fusion.84), channel_id=1, source_target_pairs={{0,4},{4,8},{8,12},{12,16},{16,20},{20,24},{24,28},{28,0},{1,5},{5... | collective-permute-start | bytes 393224 | tf_op jit(solution)/shard_map/while/body/eval_jaxpr/ppermute | solution.py:18
  245.1 23.1 %collective-permute-start = (bf16[256,256]{1,0:T(8,128)(2,1)}, bf16[256,256]{1,0:T(8,128)(2,1)}, u32[]{:S(2)}, u32[]{:S(2)}) collective-permute-start(bf16[256,256]{1,0:T(8,128)(2,1)} %copy.227), channel_id=1, source_target_pairs={{0,4},{4,8},{8,12},{12,16},{16,20},{20,24},{24,28},{28,0},{1,5},{5... | collective-permute-start | bytes 393224 | tf_op jit(solution)/shard_map/while/body/eval_jaxpr/ppermute | solution.py:18
  247.6 20.6 %collective-permute-start.1 = (bf16[256,256]{1,0:T(8,128)(2,1)}, bf16[256,256]{1,0:T(8,128)(2,1)}, u32[]{:S(2)}, u32[]{:S(2)}) collective-permute-start(bf16[256,256]{1,0:T(8,128)(2,1)} %copy.228), channel_id=1, source_target_pairs={{0,4},{4,8},{8,12},{12,16},{16,20},{20,24},{24,28},{28,0},{1,5},{5... | collective-permute-start | bytes 393224 | tf_op jit(solution)/shard_map/while/body/eval_jaxpr/ppermute | solution.py:18
  256.0 2.6 copy-start
  259.7 5.9 %collective-permute-start.3 = (bf16[256,256]{0,1:T(8,128)(2,1)S(1)}, bf16[256,256]{0,1:T(8,128)(2,1)S(1)}, u32[]{:S(2)}, u32[]{:S(2)}) collective-permute-start(bf16[256,256]{0,1:T(8,128)(2,1)S(1)} %fusion.85), channel_id=1, source_target_pairs={{0,4},{4,8},{8,12},{12,16},{16,20},{20,24},{24,28},{28,0},{1,5},{5... | collective-permute-start | bytes 393224 | tf_op jit(solution)/shard_map/while/body/eval_jaxpr/ppermute | solution.py:18
  260.8 6.7 %collective-permute-start.2 = (bf16[256,256]{0,1:T(8,128)(2,1)S(1)}, bf16[256,256]{0,1:T(8,128)(2,1)S(1)}, u32[]{:S(2)}, u32[]{:S(2)}) collective-permute-start(bf16[256,256]{0,1:T(8,128)(2,1)S(1)} %fusion.84), channel_id=1, source_target_pairs={{0,4},{4,8},{8,12},{12,16},{16,20},{20,24},{24,28},{28,0},{1,5},{5... | collective-permute-start | bytes 393224 | tf_op jit(solution)/shard_map/while/body/eval_jaxpr/ppermute | solution.py:18
  269.8 23.1 %collective-permute-start = (bf16[256,256]{1,0:T(8,128)(2,1)}, bf16[256,256]{1,0:T(8,128)(2,1)}, u32[]{:S(2)}, u32[]{:S(2)}) collective-permute-start(bf16[256,256]{1,0:T(8,128)(2,1)} %copy.227), channel_id=1, source_target_pairs={{0,4},{4,8},{8,12},{12,16},{16,20},{20,24},{24,28},{28,0},{1,5},{5... | collective-permute-start | bytes 393224 | tf_op jit(solution)/shard_map/while/body/eval_jaxpr/ppermute | solution.py:18
  273.8 19.1 %collective-permute-start.1 = (bf16[256,256]{1,0:T(8,128)(2,1)}, bf16[256,256]{1,0:T(8,128)(2,1)}, u32[]{:S(2)}, u32[]{:S(2)}) collective-permute-start(bf16[256,256]{1,0:T(8,128)(2,1)} %copy.228), channel_id=1, source_target_pairs={{0,4},{4,8},{8,12},{12,16},{16,20},{20,24},{24,28},{28,0},{1,5},{5... | collective-permute-start | bytes 393224 | tf_op jit(solution)/shard_map/while/body/eval_jaxpr/ppermute | solution.py:18
  281.1 2.6 copy-start
  284.8 5.9 %collective-permute-start.3 = (bf16[256,256]{0,1:T(8,128)(2,1)S(1)}, bf16[256,256]{0,1:T(8,128)(2,1)S(1)}, u32[]{:S(2)}, u32[]{:S(2)}) collective-permute-start(bf16[256,256]{0,1:T(8,128)(2,1)S(1)} %fusion.85), channel_id=1, source_target_pairs={{0,4},{4,8},{8,12},{12,16},{16,20},{20,24},{24,28},{28,0},{1,5},{5... | collective-permute-start | bytes 393224 | tf_op jit(solution)/shard_map/while/body/eval_jaxpr/ppermute | solution.py:18
  285.9 6.3 %collective-permute-start.2 = (bf16[256,256]{0,1:T(8,128)(2,1)S(1)}, bf16[256,256]{0,1:T(8,128)(2,1)S(1)}, u32[]{:S(2)}, u32[]{:S(2)}) collective-permute-start(bf16[256,256]{0,1:T(8,128)(2,1)S(1)} %fusion.84), channel_id=1, source_target_pairs={{0,4},{4,8},{8,12},{12,16},{16,20},{20,24},{24,28},{28,0},{1,5},{5... | collective-permute-start | bytes 393224 | tf_op jit(solution)/shard_map/while/body/eval_jaxpr/ppermute | solution.py:18
  294.5 23.6 %collective-permute-start = (bf16[256,256]{1,0:T(8,128)(2,1)}, bf16[256,256]{1,0:T(8,128)(2,1)}, u32[]{:S(2)}, u32[]{:S(2)}) collective-permute-start(bf16[256,256]{1,0:T(8,128)(2,1)} %copy.227), channel_id=1, source_target_pairs={{0,4},{4,8},{8,12},{12,16},{16,20},{20,24},{24,28},{28,0},{1,5},{5... | collective-permute-start | bytes 393224 | tf_op jit(solution)/shard_map/while/body/eval_jaxpr/ppermute | solution.py:18
  296.0 22.1 %collective-permute-start.1 = (bf16[256,256]{1,0:T(8,128)(2,1)}, bf16[256,256]{1,0:T(8,128)(2,1)}, u32[]{:S(2)}, u32[]{:S(2)}) collective-permute-start(bf16[256,256]{1,0:T(8,128)(2,1)} %copy.228), channel_id=1, source_target_pairs={{0,4},{4,8},{8,12},{12,16},{16,20},{20,24},{24,28},{28,0},{1,5},{5... | collective-permute-start | bytes 393224 | tf_op jit(solution)/shard_map/while/body/eval_jaxpr/ppermute | solution.py:18
  304.3 2.6 copy-start
  308.0 6.1 %collective-permute-start.3 = (bf16[256,256]{0,1:T(8,128)(2,1)S(1)}, bf16[256,256]{0,1:T(8,128)(2,1)S(1)}, u32[]{:S(2)}, u32[]{:S(2)}) collective-permute-start(bf16[256,256]{0,1:T(8,128)(2,1)S(1)} %fusion.85), channel_id=1, source_target_pairs={{0,4},{4,8},{8,12},{12,16},{16,20},{20,24},{24,28},{28,0},{1,5},{5... | collective-permute-start | bytes 393224 | tf_op jit(solution)/shard_map/while/body/eval_jaxpr/ppermute | solution.py:18
  310.1 7.2 %collective-permute-start.2 = (bf16[256,256]{0,1:T(8,128)(2,1)S(1)}, bf16[256,256]{0,1:T(8,128)(2,1)S(1)}, u32[]{:S(2)}, u32[]{:S(2)}) collective-permute-start(bf16[256,256]{0,1:T(8,128)(2,1)S(1)} %fusion.84), channel_id=1, source_target_pairs={{0,4},{4,8},{8,12},{12,16},{16,20},{20,24},{24,28},{28,0},{1,5},{5... | collective-permute-start | bytes 393224 | tf_op jit(solution)/shard_map/while/body/eval_jaxpr/ppermute | solution.py:18
  319.7 24.8 %collective-permute-start = (bf16[256,256]{1,0:T(8,128)(2,1)}, bf16[256,256]{1,0:T(8,128)(2,1)}, u32[]{:S(2)}, u32[]{:S(2)}) collective-permute-start(bf16[256,256]{1,0:T(8,128)(2,1)} %copy.227), channel_id=1, source_target_pairs={{0,4},{4,8},{8,12},{12,16},{16,20},{20,24},{24,28},{28,0},{1,5},{5... | collective-permute-start | bytes 393224 | tf_op jit(solution)/shard_map/while/body/eval_jaxpr/ppermute | solution.py:18
  322.6 21.9 %collective-permute-start.1 = (bf16[256,256]{1,0:T(8,128)(2,1)}, bf16[256,256]{1,0:T(8,128)(2,1)}, u32[]{:S(2)}, u32[]{:S(2)}) collective-permute-start(bf16[256,256]{1,0:T(8,128)(2,1)} %copy.228), channel_id=1, source_target_pairs={{0,4},{4,8},{8,12},{12,16},{16,20},{20,24},{24,28},{28,0},{1,5},{5... | collective-permute-start | bytes 393224 | tf_op jit(solution)/shard_map/while/body/eval_jaxpr/ppermute | solution.py:18
  331.6 2.6 copy-start
  335.4 5.9 %collective-permute-start.3 = (bf16[256,256]{0,1:T(8,128)(2,1)S(1)}, bf16[256,256]{0,1:T(8,128)(2,1)S(1)}, u32[]{:S(2)}, u32[]{:S(2)}) collective-permute-start(bf16[256,256]{0,1:T(8,128)(2,1)S(1)} %fusion.85), channel_id=1, source_target_pairs={{0,4},{4,8},{8,12},{12,16},{16,20},{20,24},{24,28},{28,0},{1,5},{5... | collective-permute-start | bytes 393224 | tf_op jit(solution)/shard_map/while/body/eval_jaxpr/ppermute | solution.py:18
  336.4 7.4 %collective-permute-start.2 = (bf16[256,256]{0,1:T(8,128)(2,1)S(1)}, bf16[256,256]{0,1:T(8,128)(2,1)S(1)}, u32[]{:S(2)}, u32[]{:S(2)}) collective-permute-start(bf16[256,256]{0,1:T(8,128)(2,1)S(1)} %fusion.84), channel_id=1, source_target_pairs={{0,4},{4,8},{8,12},{12,16},{16,20},{20,24},{24,28},{28,0},{1,5},{5... | collective-permute-start | bytes 393224 | tf_op jit(solution)/shard_map/while/body/eval_jaxpr/ppermute | solution.py:18
  346.1 24.5 %collective-permute-start = (bf16[256,256]{1,0:T(8,128)(2,1)}, bf16[256,256]{1,0:T(8,128)(2,1)}, u32[]{:S(2)}, u32[]{:S(2)}) collective-permute-start(bf16[256,256]{1,0:T(8,128)(2,1)} %copy.227), channel_id=1, source_target_pairs={{0,4},{4,8},{8,12},{12,16},{16,20},{20,24},{24,28},{28,0},{1,5},{5... | collective-permute-start | bytes 393224 | tf_op jit(solution)/shard_map/while/body/eval_jaxpr/ppermute | solution.py:18
  349.4 21.2 %collective-permute-start.1 = (bf16[256,256]{1,0:T(8,128)(2,1)}, bf16[256,256]{1,0:T(8,128)(2,1)}, u32[]{:S(2)}, u32[]{:S(2)}) collective-permute-start(bf16[256,256]{1,0:T(8,128)(2,1)} %copy.228), channel_id=1, source_target_pairs={{0,4},{4,8},{8,12},{12,16},{16,20},{20,24},{24,28},{28,0},{1,5},{5... | collective-permute-start | bytes 393224 | tf_op jit(solution)/shard_map/while/body/eval_jaxpr/ppermute | solution.py:18
  358.0 2.6 copy-start
  361.7 6.7 %collective-permute-start.3 = (bf16[256,256]{0,1:T(8,128)(2,1)S(1)}, bf16[256,256]{0,1:T(8,128)(2,1)S(1)}, u32[]{:S(2)}, u32[]{:S(2)}) collective-permute-start(bf16[256,256]{0,1:T(8,128)(2,1)S(1)} %fusion.85), channel_id=1, source_target_pairs={{0,4},{4,8},{8,12},{12,16},{16,20},{20,24},{24,28},{28,0},{1,5},{5... | collective-permute-start | bytes 393224 | tf_op jit(solution)/shard_map/while/body/eval_jaxpr/ppermute | solution.py:18
  362.8 7.1 %collective-permute-start.2 = (bf16[256,256]{0,1:T(8,128)(2,1)S(1)}, bf16[256,256]{0,1:T(8,128)(2,1)S(1)}, u32[]{:S(2)}, u32[]{:S(2)}) collective-permute-start(bf16[256,256]{0,1:T(8,128)(2,1)S(1)} %fusion.84), channel_id=1, source_target_pairs={{0,4},{4,8},{8,12},{12,16},{16,20},{20,24},{24,28},{28,0},{1,5},{5... | collective-permute-start | bytes 393224 | tf_op jit(solution)/shard_map/while/body/eval_jaxpr/ppermute | solution.py:18
  372.2 23.0 %collective-permute-start = (bf16[256,256]{1,0:T(8,128)(2,1)}, bf16[256,256]{1,0:T(8,128)(2,1)}, u32[]{:S(2)}, u32[]{:S(2)}) collective-permute-start(bf16[256,256]{1,0:T(8,128)(2,1)} %copy.227), channel_id=1, source_target_pairs={{0,4},{4,8},{8,12},{12,16},{16,20},{20,24},{24,28},{28,0},{1,5},{5... | collective-permute-start | bytes 393224 | tf_op jit(solution)/shard_map/while/body/eval_jaxpr/ppermute | solution.py:18
  373.8 21.4 %collective-permute-start.1 = (bf16[256,256]{1,0:T(8,128)(2,1)}, bf16[256,256]{1,0:T(8,128)(2,1)}, u32[]{:S(2)}, u32[]{:S(2)}) collective-permute-start(bf16[256,256]{1,0:T(8,128)(2,1)} %copy.228), channel_id=1, source_target_pairs={{0,4},{4,8},{8,12},{12,16},{16,20},{20,24},{24,28},{28,0},{1,5},{5... | collective-permute-start | bytes 393224 | tf_op jit(solution)/shard_map/while/body/eval_jaxpr/ppermute | solution.py:18
  382.2 2.6 copy-start
  386.0 7.1 %collective-permute-start.3 = (bf16[256,256]{0,1:T(8,128)(2,1)S(1)}, bf16[256,256]{0,1:T(8,128)(2,1)S(1)}, u32[]{:S(2)}, u32[]{:S(2)}) collective-permute-start(bf16[256,256]{0,1:T(8,128)(2,1)S(1)} %fusion.85), channel_id=1, source_target_pairs={{0,4},{4,8},{8,12},{12,16},{16,20},{20,24},{24,28},{28,0},{1,5},{5... | collective-permute-start | bytes 393224 | tf_op jit(solution)/shard_map/while/body/eval_jaxpr/ppermute | solution.py:18
  387.4 7.0 %collective-permute-start.2 = (bf16[256,256]{0,1:T(8,128)(2,1)S(1)}, bf16[256,256]{0,1:T(8,128)(2,1)S(1)}, u32[]{:S(2)}, u32[]{:S(2)}) collective-permute-start(bf16[256,256]{0,1:T(8,128)(2,1)S(1)} %fusion.84), channel_id=1, source_target_pairs={{0,4},{4,8},{8,12},{12,16},{16,20},{20,24},{24,28},{28,0},{1,5},{5... | collective-permute-start | bytes 393224 | tf_op jit(solution)/shard_map/while/body/eval_jaxpr/ppermute | solution.py:18
  396.8 25.7 %collective-permute-start = (bf16[256,256]{1,0:T(8,128)(2,1)}, bf16[256,256]{1,0:T(8,128)(2,1)}, u32[]{:S(2)}, u32[]{:S(2)}) collective-permute-start(bf16[256,256]{1,0:T(8,128)(2,1)} %copy.227), channel_id=1, source_target_pairs={{0,4},{4,8},{8,12},{12,16},{16,20},{20,24},{24,28},{28,0},{1,5},{5... | collective-permute-start | bytes 393224 | tf_op jit(solution)/shard_map/while/body/eval_jaxpr/ppermute | solution.py:18
  400.6 21.9 %collective-permute-start.1 = (bf16[256,256]{1,0:T(8,128)(2,1)}, bf16[256,256]{1,0:T(8,128)(2,1)}, u32[]{:S(2)}, u32[]{:S(2)}) collective-permute-start(bf16[256,256]{1,0:T(8,128)(2,1)} %copy.228), channel_id=1, source_target_pairs={{0,4},{4,8},{8,12},{12,16},{16,20},{20,24},{24,28},{28,0},{1,5},{5... | collective-permute-start | bytes 393224 | tf_op jit(solution)/shard_map/while/body/eval_jaxpr/ppermute | solution.py:18
  407.9 2.6 copy-start
  411.6 8.7 %collective-permute-start.3 = (bf16[256,256]{0,1:T(8,128)(2,1)S(1)}, bf16[256,256]{0,1:T(8,128)(2,1)S(1)}, u32[]{:S(2)}, u32[]{:S(2)}) collective-permute-start(bf16[256,256]{0,1:T(8,128)(2,1)S(1)} %fusion.85), channel_id=1, source_target_pairs={{0,4},{4,8},{8,12},{12,16},{16,20},{20,24},{24,28},{28,0},{1,5},{5... | collective-permute-start | bytes 393224 | tf_op jit(solution)/shard_map/while/body/eval_jaxpr/ppermute | solution.py:18
  412.7 9.0 %collective-permute-start.2 = (bf16[256,256]{0,1:T(8,128)(2,1)S(1)}, bf16[256,256]{0,1:T(8,128)(2,1)S(1)}, u32[]{:S(2)}, u32[]{:S(2)}) collective-permute-start(bf16[256,256]{0,1:T(8,128)(2,1)S(1)} %fusion.84), channel_id=1, source_target_pairs={{0,4},{4,8},{8,12},{12,16},{16,20},{20,24},{24,28},{28,0},{1,5},{5... | collective-permute-start | bytes 393224 | tf_op jit(solution)/shard_map/while/body/eval_jaxpr/ppermute | solution.py:18
  423.7 10.3 %all-to-all-start.5 = ((bf16[8,64,256]{2,1,0:T(8,128)(2,1)}), bf16[8,64,256]{2,1,0:T(8,128)(2,1)S(1)}, u32[]{:S(2)}, u32[]{:S(2)}) async-start(bf16[8,64,256]{2,1,0:T(8,128)(2,1)} %copy.132), calls=%async_computation.5 | async-start | bytes 524288 | tf_op jit(solution)/shard_map/all_to_all | solution.py:243
  434.0 15.6 %all-to-all-start.4 = ((bf16[8,64,256]{2,1,0:T(8,128)(2,1)}), bf16[8,64,256]{2,1,0:T(8,128)(2,1)S(1)}, u32[]{:S(2)}, u32[]{:S(2)}) async-start(bf16[8,64,256]{2,1,0:T(8,128)(2,1)} %copy.127), calls=%async_computation.4 | async-start | bytes 524288 | tf_op jit(solution)/shard_map/all_to_all | solution.py:240
  439.7 16.6 %copy-start.7 = (s32[4]{0:T(128)S(1)}, s32[4]{0:T(128)}, u32[]{:S(2)}) copy-start(s32[4]{0:T(128)} %copy-done.6) | copy-start | bytes 52
  449.5 19.9 %all-to-all-start.3 = ((bf16[8,64,1024]{2,1,0:T(8,128)(2,1)}), bf16[8,64,1024]{2,1,0:T(8,128)(2,1)S(1)}, u32[]{:S(2)}, u32[]{:S(2)}) async-start(bf16[8,64,1024]{2,1,0:T(8,128)(2,1)} %copy.122), calls=%async_computation.3 | async-start | bytes 2097152 | tf_op jit(solution)/shard_map/all_to_all | solution.py:237
  456.3 88.4 %reduce-scatter.2.cloned.1.call-start = ((), (), s32[]{:S(2)}) async-start(), calls=%async_computation.10 | async-start | bytes 5242880 | tf_op jit(solution)/shard_map/reduce_scatter | solution.py:262
  489.3 6.1 %copy-start.3 = (bf16[8192,256]{1,0:T(8,128)(2,1)S(1)}, bf16[8192,256]{1,0:T(8,128)(2,1)}, u32[]{:S(2)}) copy-start(bf16[8192,256]{1,0:T(8,128)(2,1)} %param.18) | copy-start | bytes 12582916
  498.6 1.0 copy-start.4
  (2 other events, 1.9 us)
Sparse Core Ops, SparseCore 0:
  9.6 35.5 all-gather.3
  72.8 49.1 all-gather.7
  124.2 39.0 all-gather.5
  498.8 45.8 reduce-scatter.1
where the time goes:
time: 556 us; the launch traced here: 551 us
  waiting for transfers between devices  198 us (36%)
  matrix products  104 us (19%)
  local copies, waits for them, and re-layouts  90.9 us (16%)
  starting transfers between devices  87.5 us (16%)
  other arithmetic  49 us (9%)
  between operations  14.1 us (3%)
  loops' own time  8.2 us (1%)
    ppermute x32, starting transfers between devices, from_behind(): return lax.ppermute(value, axis, pairs)  53 us
    reduce_scatter x1, waiting for transfers between devices, per_device(): lax.psum_scatter(grad_terms.astype(jnp.bfloat16), 'heads', scatter_dimens...  43.4 us
    all_gather x1, waiting for transfers between devices, per_device(): key_piece = lax.all_gather(ctx_k, 'ctx', axis=0, tiled=True)  37.9 us
    all_gather x1, waiting for transfers between devices, per_device(): piece = lax.all_gather(activations, 'heads', axis=1, tiled=True)  35.5 us
    ppermute x32, waiting for transfers between devices, from_behind(): return lax.ppermute(value, axis, pairs)  31.2 us
    dot_general x3, matrix products, transposed_dot(): lax.dot_general(left, weight, (((1,), (1,)), ((), ())), preferred_element...  28.3 us
    while x16, local copies, waits for them, and re-layouts  25 us
    all_to_all x1, waiting for transfers between devices, per_device(): lax.all_to_all(spread(send_map, loader_q, block_rows), 'ctx', split_axis=...  24.2 us
  transfers between devices with their start and end apart: 42, of which 23 were waited for; matrix products, arithmetic and copies ran while one was open for 26% of the time, Pallas kernels for 0%

commit v1 on v0

v1 whole, which is shorter than its diff:
```python
import functools
import math

import jax
import jax.numpy as jnp
from jax import lax
from jax.experimental import pallas as pl
from jax.experimental.pallas import tpu as pltpu
from jax.sharding import PartitionSpec as P

HD = 128
QPK = 4
NEG = -1e30
BF = jnp.bfloat16
F32 = jnp.float32


def layout(block_dest):
    nblk = block_dest.shape[0]
    index = jnp.arange(nblk, dtype=jnp.int32)
    order_key = block_dest * nblk + index
    ranks = jnp.sum((order_key[None, :] < order_key[:, None]).astype(jnp.int32), axis=1)
    return jnp.sum(jnp.where(ranks[None, :] == index[:, None], index[None, :], 0), axis=1)


def spread(table, array, block_rows):
    width = array.shape[-1]
    grouped = array.reshape(table.shape[1], block_rows * width)
    moved = jnp.dot(table, grouped, preferred_element_type=F32)
    return moved.astype(BF).reshape(table.shape[0], block_rows, width)


def dot_nt(a, b):
    return lax.dot_general(a, b, (((1,), (1,)), ((), ())), preferred_element_type=F32)


def dot_tn(a, b):
    return lax.dot_general(a, b, (((0,), (0,)), ((), ())), preferred_element_type=F32)


def dot_nn(a, b):
    return jnp.dot(a, b, preferred_element_type=F32)


def bias_of(start, rank, keys):
    rows = start.shape[0]
    qpos = rank * rows + lax.broadcasted_iota(jnp.int32, (rows, keys), 0)
    col = lax.broadcasted_iota(jnp.int32, (rows, keys), 1)
    slot = col // rows
    kpos = (rank - 2 * slot) * rows + col
    seen = (kpos <= qpos) & (kpos >= start)
    return jnp.where(seen, 0.0, NEG)


def attend_head(h, q_ref, kv_ref, g_ref, bias_ref, att_ref, dq_ref, dkv_ref, first):
    scale = 1.0 / math.sqrt(HD)
    half = kv_ref.shape[1] // 2
    hs = slice(h * HD, (h + 1) * HD)
    g = h // QPK
    ks = slice(g * HD, (g + 1) * HD)
    vs = slice(half + g * HD, half + (g + 1) * HD)
    q = q_ref[:, hs]
    go = g_ref[:, hs]
    k = kv_ref[:, ks]
    v = kv_ref[:, vs]
    s = dot_nt(q, k) * scale + bias_ref[...]
    m = jnp.max(s, axis=1, keepdims=True)
    p = jnp.exp(s - m)
    w = p * (1.0 / jnp.sum(p, axis=1, keepdims=True))
    wb = w.astype(BF)
    low = (w - wb.astype(F32)).astype(BF)
    att = (dot_nn(wb, v) + dot_nn(low, v)).astype(BF)
    att_ref[:, hs] = att
    delta = jnp.sum(go.astype(F32) * att.astype(F32), axis=1, keepdims=True)
    ds = (w * (dot_nt(go, v) - delta) * scale).astype(BF)
    dq_ref[:, hs] = dot_nn(ds, k).astype(BF)
    dk = dot_tn(ds, q)
    dv = dot_tn(wb, go)
    if first:
        dkv_ref[:, ks] = dk
        dkv_ref[:, vs] = dv
    else:
        dkv_ref[:, ks] += dk
        dkv_ref[:, vs] += dv


def attn_kernel(heads, start_ref, q_ref, kv_ref, g_ref, att_ref, dq_ref, dkv_ref, bias_ref, sum_ref):
    rank = lax.axis_index("ctx")
    bias_ref[...] = bias_of(start_ref[...], rank, kv_ref.shape[0])
    for h in range(heads):
        attend_head(h, q_ref, kv_ref, g_ref, bias_ref, att_ref, dq_ref, sum_ref, h % QPK == 0)
    dkv_ref[...] = sum_ref[...].astype(BF)


def attention(start, q, kv, g):
    keys = kv.shape[0]
    rows, width = q.shape
    vm = pl.BlockSpec(memory_space=pltpu.VMEM)
    return pl.pallas_call(
        functools.partial(attn_kernel, width // HD),
        out_shape=(
            jax.ShapeDtypeStruct((rows, width), BF),
            jax.ShapeDtypeStruct((rows, width), BF),
            jax.ShapeDtypeStruct(kv.shape, BF),
        ),
        in_specs=[vm] * 4,
        out_specs=(vm,) * 3,
        scratch_shapes=[pltpu.VMEM((rows, keys), F32), pltpu.VMEM(kv.shape, F32)],
        compiler_params=pltpu.CompilerParams(vmem_limit_bytes=40 * 2**20),
        name="attention",
    )(start, q, kv, g)


def shift(value, steps):
    count = lax.axis_size("ctx")
    pairs = [(s, s + steps) for s in range(count) if 0 <= s + steps < count]
    return lax.ppermute(value, "ctx", pairs)


def per_device(activations, w_query, w_key, w_value, doc_lengths, block_dest, out_grad):
    ctx_count = lax.axis_size("ctx")
    ctx_rank = lax.axis_index("ctx")
    tok_dev = activations.shape[0]
    nblk = block_dest.shape[0]
    block_rows = tok_dev * ctx_count // nblk
    blocks_here = tok_dev // block_rows
    ctx_blocks = layout(block_dest)
    slots = jnp.arange(ctx_count, dtype=jnp.int32)
    my_dest = lax.dynamic_slice_in_dim(block_dest, ctx_rank * blocks_here, blocks_here, 0)
    send_map = (my_dest[None, :] == slots[:, None]).astype(BF)
    mine = lax.dynamic_slice_in_dim(ctx_blocks, ctx_rank * blocks_here, blocks_here, 0)
    take_map = ((mine // blocks_here)[:, None] == slots[None, :]).astype(BF)
    ends = jnp.cumsum(doc_lengths)
    my_pos = ctx_rank * tok_dev + jnp.arange(tok_dev, dtype=jnp.int32)
    start = jnp.max(jnp.where(ends[None, :] <= my_pos[:, None], ends[None, :], 0), axis=1)[:, None]

    def exchange(table_out, value, table_in):
        sent = lax.all_to_all(
            spread(table_out, value, block_rows), "ctx", split_axis=0, concat_axis=0, tiled=True
        )
        return spread(table_in, sent, block_rows).reshape(tok_dev, -1)

    grad = exchange(take_map.T, out_grad, send_map.T)
    piece = lax.all_gather(activations, "heads", axis=1, tiled=True)
    k = dot_nn(piece, w_key).astype(BF)
    v = dot_nn(piece, w_value).astype(BF)
    kv = jnp.concatenate([k, v], axis=1)
    back = ctx_count // 2
    kvs = jnp.concatenate([kv] + [shift(kv, j) for j in range(1, back + 1)], axis=0)
    q = dot_nn(piece, w_query).astype(BF)
    att, dq, dkvs = attention(start, q, kvs, grad)
    out = exchange(send_map, att, take_map)
    total = dkvs[:tok_dev].astype(F32)
    for j in range(1, back + 1):
        total = total + shift(dkvs[j * tok_dev : (j + 1) * tok_dev], -j).astype(F32)
    dkv = total.astype(BF)
    half = dkv.shape[1] // 2
    terms = dot_nt(dq, w_query) + dot_nt(dkv[:, :half], w_key) + dot_nt(dkv[:, half:], w_value)
    input_grad = lax.psum_scatter(terms.astype(BF), "heads", scatter_dimension=1, tiled=True)
    return (out, input_grad)


def solution(mesh):
    return jax.shard_map(
        per_device,
        mesh=mesh,
        in_specs=(
            P("ctx", "heads"),
            P(None, "heads"),
            P(None, "heads"),
            P(None, "heads"),
            P(),
            P(),
            P("ctx", "heads"),
        ),
        out_specs=(P("ctx", "heads"), P("ctx", "heads")),
        check_vma=False,
    )
```

time: 556 us -> 217 us (0.39)
  waiting for transfers between devices: 198 us -> 79 us
  local copies, waits for them, and re-layouts: 90.9 us -> 7.16 us
  matrix products: 104 us -> 42 us
  starting transfers between devices: 87.5 us -> 28 us
  other arithmetic: 49 us -> 1.52 us
  blocking collectives: 0 us -> 29.1 us
  Pallas kernels: 0 us -> 13.8 us
  loops' own time: 8.2 us -> 0 us
    dot_general x66 -> x10, matrix products: 104 us -> 42 us  [the longest x3 24.2 us: dot_nt(): lax.dot_general(a, b, (((1,), (1,)), ((), ())), preferred_element_type=F32)]
    all_gather x2 -> x0, waiting for transfers between devices: 37.9 us -> none  [the longest x1 37.9 us: per_device(): key_piece = lax.all_gather(ctx_k, 'ctx', axis=0, tiled=True)]
    all_gather x1, waiting for transfers between devices: 35.5 us -> 2.48 us  [per_device(): piece = lax.all_gather(activations, 'heads', axis=1, tiled=True)]
    reduce_scatter x1, waiting for transfers between devices: 43.4 us -> 11 us  [per_device(): lax.psum_scatter(terms.astype(BF), 'heads', scatter_dimension=1, tiled=True)]
    ppermute x32 -> x8, starting transfers between devices: 53 us -> 21.8 us  [shift(): return lax.ppermute(value, 'ctx', pairs)]
    while x21 -> x0, local copies, waits for them, and re-layouts: 30.2 us -> none
    all_to_all x0 -> x1, blocking collectives: none -> 29.1 us  [exchange(): lax.all_to_all(spread(table_out, value, block_rows), 'ctx', split_axis=0,...]
    all_to_all x6 -> x1, starting transfers between devices: 34.4 us -> 6.14 us  [exchange(): lax.all_to_all(spread(table_out, value, block_rows), 'ctx', split_axis=0,...]
  transfers between devices with their start and end apart: 42 -> 11, of which waited for: 23 -> 8; matrix products, arithmetic and copies ran while one was open for 26% -> 8% of each run, Pallas kernels for 0% -> 0%
where the time goes in v1:
time: 217 us; the launch traced here: 215 us
  waiting for transfers between devices  79 us (36%)
  matrix products  42 us (19%)
  blocking collectives  29.1 us (13%)
  starting transfers between devices  28 us (13%)
  between operations  14.4 us (7%)
  Pallas kernels  13.8 us (6%)
  local copies, waits for them, and re-layouts  7.16 us (3%)
    ppermute x8, waiting for transfers between devices, shift(): return lax.ppermute(value, 'ctx', pairs)  42.8 us
    all_to_all x1, blocking collectives, exchange(): lax.all_to_all(spread(table_out, value, block_rows), 'ctx', split_axis=0,...  29.1 us
    dot_general x3, matrix products, dot_nt(): lax.dot_general(a, b, (((1,), (1,)), ((), ())), preferred_element_type=F32)  24.2 us
    all_to_all x1, waiting for transfers between devices, exchange(): lax.all_to_all(spread(table_out, value, block_rows), 'ctx', split_axis=0,...  22 us
    ppermute x8, starting transfers between devices, shift(): return lax.ppermute(value, 'ctx', pairs)  21.8 us
    dot_general x3, matrix products, dot_nn(): return jnp.dot(a, b, preferred_element_type=F32)  15.8 us
    pallas_call x1, Pallas kernels, attention(): pl.pallas_call(functools.partial(attn_kernel, width // HD), out_shape=(ja...  13.8 us
    reduce_scatter x1, waiting for transfers between devices, per_device(): lax.psum_scatter(terms.astype(BF), 'heads', scatter_dimension=1, tiled=True)  11 us
  transfers between devices with their start and end apart: 11, of which 8 were waited for; matrix products, arithmetic and copies ran while one was open for 8% of the time, Pallas kernels for 0%

profile of v1, /device:TPU:16, one launch (start us, length us, event | category | flops | bytes accessed | tf_op | source)
XLA Modules:
  0.0 214.9 jit_solution(3131959520755417021)
XLA Ops:
  7.2 0.0 copy-start.3
  7.2 0.0 copy-start.4
  7.2 0.0 all-gather.2.cloned.1.call-start
  7.2 0.7 all-gather.2.cloned.1.call-update
  7.9 1.4 reshape.57
  9.4 0.7 iota_add_fusion.1
  10.0 0.2 convert_reduce_fusion
  10.2 0.1 select_reduce_fusion
  10.3 0.1 and_select_fusion
  10.4 0.6 convolution_convert_fusion.1
  11.0 1.5 copy.21
  12.6 6.1 %all-to-all-start = ((bf16[8,64,1024]{2,1,0:T(8,128)(2,1)}), bf16[8,64,1024]{2,1,0:T(8,128)(2,1)S(1)}, u32[]{:S(2)}, u32[]{:S(2)}) async-start(bf16[8,64,1024]{2,1,0:T(8,128)(2,1)} %copy.21), calls=%async_computation | async-start | bytes 2097152 | tf_op jit(solution)/shard_map/all_to_all | solution.py:138
  18.7 0.0 reduce-scatter.2.cloned.1.call-start
  18.7 0.0 copy-done.3
  18.7 0.1 dynamic_slice.7
  18.8 0.0 copy-done.4
  18.8 0.2 reduce-window.8
  19.0 0.1 select_reduce_fusion.1
  19.1 0.1 copy.22.start_ref
  19.2 22.0 %all-to-all-done = bf16[8,64,1024]{2,1,0:T(8,128)(2,1)S(1)} async-done(((bf16[8,64,1024]{2,1,0:T(8,128)(2,1)}), bf16[8,64,1024]{2,1,0:T(8,128)(2,1)S(1)}, u32[]{:S(2)}, u32[]{:S(2)}) %all-to-all-start) | async-done | bytes 1048608 | tf_op jit(solution)/shard_map/all_to_all | solution.py:138
  41.2 0.6 copy.26
  41.8 0.5 convolution_convert_fusion.3
  42.3 0.4 reshape_reshape.6.g_ref
  42.7 2.5 %all-gather.2.cloned.1.call-done = bf16[256,8192]{1,0:T(8,128)(2,1)} async-done(((bf16[256,2048]{1,0:T(8,128)(2,1)}), bf16[256,8192]{1,0:T(8,128)(2,1)}) %all-gather.2.cloned.1.call-update) | async-done | bytes 4194320 | tf_op jit(solution)/shard_map/all_gather | solution.py:144
  45.2 4.8 %convolution_convert_fusion.5 = bf16[256,256]{1,0:T(8,128)(2,1)S(1)} fusion(bf16[256,8192]{1,0:T(8,128)(2,1)} %all-gather.2.cloned.1.call-done, bf16[8192,256]{1,0:T(8,128)(2,1)} %param.10), kind=kOutput, calls=%fused_computation.8 | convolution fusion | flops 1073807360 | bytes 8519680 | tf_op jit(solution)/shard_map/dot_general | solution.py:42
  50.0 0.0 copy-done.1
  50.0 0.0 slice-start.2
  50.1 0.0 slice-start.3
  50.1 4.3 %convolution_convert_fusion.6 = bf16[256,256]{1,0:T(8,128)(2,1)S(1)} fusion(bf16[256,8192]{1,0:T(8,128)(2,1)} %all-gather.2.cloned.1.call-done, bf16[8192,256]{1,0:T(8,128)(2,1)S(1)} %copy-done.1), kind=kOutput, calls=%fused_computation.9 | convolution fusion | flops 1073807360 | bytes 8519680 | tf_op jit(solution)/shard_map/dot_general | solution.py:42
  54.4 4.4 %collective-permute-start.2 = (bf16[256,512]{1,0:T(8,128)(2,1)S(1)}, bf16[256,512]{1,0:T(8,128)(2,1)S(1)}, u32[]{:S(2)}, u32[]{:S(2)}) collective-permute-start(bf16[256,512]{1,0:T(8,128)(2,1)S(1)} %get-tuple-element.12), channel_id=1, source_target_pairs={{0,12},{4,16},{8,20},{12,24},{16,28},{1,13},{5,17},{9,21},{13,25},... | collective-permute-start | bytes 786440 | tf_op jit(solution)/shard_map/ppermute | solution.py:117
  58.9 1.9 collective-permute-start.1
  60.8 1.9 collective-permute-start
  62.7 1.5 collective-permute-start.3
  64.2 0.0 slice-done
  64.3 6.7 %convolution_convert_fusion.4.q_ref = bf16[256,1024]{1,0:T(8,128)(2,1)S(1)} fusion(bf16[256,8192]{1,0:T(8,128)(2,1)} %all-gather.2.cloned.1.call-done, bf16[8192,1024]{1,0:T(8,128)(2,1)S(1)} %bitcast.24), kind=kOutput, calls=%fused_computation.7 | convolution fusion | flops 4295229440 | bytes 21495808 | tf_op jit(solution)/shard_map/dot_general | solution.py:42
  70.9 0.0 copy-start
  70.9 18.4 %collective-permute-done = bf16[256,512]{1,0:T(8,128)(2,1)S(1)} collective-permute-done((bf16[256,512]{1,0:T(8,128)(2,1)S(1)}, bf16[256,512]{1,0:T(8,128)(2,1)S(1)}, u32[]{:S(2)}, u32[]{:S(2)}) %collective-permute-start) | collective-permute-done | bytes 262176 | tf_op jit(solution)/shard_map/ppermute | solution.py:117
  89.3 0.0 collective-permute-done.1
  89.4 0.0 collective-permute-done.2
  89.4 0.0 collective-permute-done.3
  89.4 13.8 %attention.1 = (bf16[256,1024]{1,0:T(8,128)(2,1)S(1)}, bf16[256,1024]{1,0:T(8,128)(2,1)S(1)}, bf16[1280,512]{1,0:T(8,128)(2,1)S(1)}) custom-call(s32[256,1]{1,0:T(8,128)S(1)} %copy.22.start_ref, bf16[256,1024]{1,0:T(8,128)(2,1)S(1)} %convolution_convert_fusion.4.q_ref, bf16[1280,512]{1,0:T(8,128)(2,1)S(1)} %constant_dynamic-update-slice_fusion.kv_ref, ...), custom_call_target="tpu_custom_call" | custom-call | tf_op jit(solution)/shard_map/attention/pallas_call | solution.py:99
  103.3 0.1 fusion.10
  103.3 6.9 %collective-permute-start.4 = (bf16[256,512]{1,0:T(8,128)(2,1)S(1)}, bf16[256,512]{1,0:T(8,128)(2,1)S(1)}, u32[]{:S(2)}, u32[]{:S(2)}) collective-permute-start(bf16[256,512]{1,0:T(8,128)(2,1)S(1)} %get-tuple-element.8), channel_id=1, source_target_pairs={{4,0},{8,4},{12,8},{16,12},{20,16},{24,20},{28,24},{5,1},{9,5},{13... | collective-permute-start | bytes 786440 | tf_op jit(solution)/shard_map/ppermute | solution.py:117
  110.2 1.3 collective-permute-start.7
  111.6 1.9 collective-permute-start.6
  113.5 1.9 collective-permute-start.5
  115.4 7.6 %collective-permute-done.4 = bf16[256,512]{1,0:T(8,128)(2,1)S(1)} collective-permute-done((bf16[256,512]{1,0:T(8,128)(2,1)S(1)}, bf16[256,512]{1,0:T(8,128)(2,1)S(1)}, u32[]{:S(2)}, u32[]{:S(2)}) %collective-permute-start.4) | collective-permute-done | bytes 262176 | tf_op jit(solution)/shard_map/ppermute | solution.py:117
  123.0 5.6 %collective-permute-done.7 = bf16[256,512]{1,0:T(8,128)(2,1)S(1)} collective-permute-done((bf16[256,512]{1,0:T(8,128)(2,1)S(1)}, bf16[256,512]{1,0:T(8,128)(2,1)S(1)}, u32[]{:S(2)}, u32[]{:S(2)}) %collective-permute-start.7) | collective-permute-done | bytes 262176 | tf_op jit(solution)/shard_map/ppermute | solution.py:117
  128.7 5.6 %collective-permute-done.6 = bf16[256,512]{1,0:T(8,128)(2,1)S(1)} collective-permute-done((bf16[256,512]{1,0:T(8,128)(2,1)S(1)}, bf16[256,512]{1,0:T(8,128)(2,1)S(1)}, u32[]{:S(2)}, u32[]{:S(2)}) %collective-permute-start.6) | collective-permute-done | bytes 262176 | tf_op jit(solution)/shard_map/ppermute | solution.py:117
  134.3 5.5 %collective-permute-done.5 = bf16[256,512]{1,0:T(8,128)(2,1)S(1)} collective-permute-done((bf16[256,512]{1,0:T(8,128)(2,1)S(1)}, bf16[256,512]{1,0:T(8,128)(2,1)S(1)}, u32[]{:S(2)}, u32[]{:S(2)}) %collective-permute-start.5) | collective-permute-done | bytes 262176 | tf_op jit(solution)/shard_map/ppermute | solution.py:117
  139.8 0.2 add_convert_fusion
  140.0 0.0 copy-start.2
  140.0 4.5 %fusion.2 = f32[256,8192]{1,0:T(8,128)} fusion(bf16[8192,256]{1,0:T(8,128)(2,1)S(1)} %copy-done, bf16[256,512]{1,0:T(8,128)(2,1)S(1)} %add_convert_fusion), kind=kOutput, calls=%fused_computation.12 | convolution fusion | flops 1073741824 | bytes 12713984 | tf_op jit(solution)/shard_map/dot_general | solution.py:34
  144.5 4.5 %fusion.4 = f32[256,8192]{1,0:T(8,128)} fusion(bf16[8192,256]{1,0:T(8,128)(2,1)S(1)} %copy-done.2, bf16[256,512]{1,0:T(8,128)(2,1)S(1)} %add_convert_fusion), kind=kOutput, calls=%fused_computation.14 | convolution fusion | flops 1073741824 | bytes 12713984 | tf_op jit(solution)/shard_map/dot_general | solution.py:34
  149.1 15.1 %fusion.1 = bf16[256,8192]{1,0:T(8,128)(2,1)} fusion(f32[256,8192]{1,0:T(8,128)} %fusion.2, f32[256,8192]{1,0:T(8,128)} %fusion.4, bf16[256,1024]{1,0:T(8,128)(2,1)S(1)} %get-tuple-element.6, bf16[8192,1024]{1,0:T(8,128)(2,1)} %param.8), kind=kOutput, calls=%fused_computation.6 | convolution fusion | flops 4301258752 | bytes 38273024 | tf_op jit(solution)/shard_map/dot_general | solution.py:34
  164.2 0.0 reduce-scatter.2.cloned.1.call-update
  164.2 0.4 reshape.60
  164.6 0.4 convolution_convert_fusion
  165.1 0.6 copy.23
  165.6 29.1 %all_to_all.10 = bf16[8,64,1024]{2,1,0:T(8,128)(2,1)S(1)} all-to-all(bf16[8,64,1024]{2,1,0:T(8,128)(2,1)S(1)} %copy.23), channel_id=1, replica_groups=mesh['ctx'=8,'heads'=4] {'ctx'}, dimensions={0} | all-to-all | bytes 2097152 | tf_op jit(solution)/shard_map/all_to_all | solution.py:138
  194.8 0.6 copy.27
  195.3 0.5 convolution_convert_fusion.2
  195.8 1.2 reshape_reshape.7
  197.0 11.0 %reduce-scatter.2.cloned.1.call-done = bf16[256,2048]{1,0:T(8,128)(2,1)} async-done(((bf16[256,8192]{1,0:T(8,128)(2,1)}), bf16[256,2048]{1,0:T(8,128)(2,1)}) %reduce-scatter.2.cloned.1.call-update) | async-done | bytes 1048592 | tf_op jit(solution)/shard_map/reduce_scatter | solution.py:159
  (15 shorter events, 0.1 us)
Async XLA Ops:
  7.2 11.5 %copy-start.3 = (s32[32]{0:T(128)S(1)}, s32[32]{0:T(128)}, u32[]{:S(2)}) copy-start(s32[32]{0:T(128)} %param.12) | copy-start | bytes 388
  7.2 11.6 %copy-start.4 = (s32[8]{0:T(128)S(1)}, s32[8]{0:T(128)}, u32[]{:S(2)}) copy-start(s32[8]{0:T(128)} %param.11) | copy-start | bytes 100
  7.2 38.0 %all-gather.2.cloned.1.call-start = ((), (), s32[]{:S(2)}) async-start(), calls=%async_computation.3 | async-start | bytes 5242880 | tf_op jit(solution)/shard_map/all_gather | solution.py:144
  12.6 28.6 %all-to-all-start = ((bf16[8,64,1024]{2,1,0:T(8,128)(2,1)}), bf16[8,64,1024]{2,1,0:T(8,128)(2,1)S(1)}, u32[]{:S(2)}, u32[]{:S(2)}) async-start(bf16[8,64,1024]{2,1,0:T(8,128)(2,1)} %copy.21), calls=%async_computation | async-start | bytes 2097152 | tf_op jit(solution)/shard_map/all_to_all | solution.py:138
  18.7 189.4 %reduce-scatter.2.cloned.1.call-start = ((), (), s32[]{:S(2)}) async-start(), calls=%async_computation.4 | async-start | bytes 5242880 | tf_op jit(solution)/shard_map/reduce_scatter | solution.py:159
  45.2 4.9 %copy-start.1 = (bf16[8192,256]{1,0:T(8,128)(2,1)S(1)}, bf16[8192,256]{1,0:T(8,128)(2,1)}, u32[]{:S(2)}) copy-start(bf16[8192,256]{1,0:T(8,128)(2,1)} %param.9) | copy-start | bytes 12582916
  45.2 19.0 %slice-start = ((s8[16777216]{0:T(1024)(128)(4,1)}), s8[4194304]{0:T(1024)(128)(4,1)S(1)}, s32[]{:S(2)}) async-start(s8[16777216]{0:T(1024)(128)(4,1)} %bitcast.23), calls=%async_computation.5 | async-start | bytes 8388608
  45.2 19.0 %slice-start.1 = ((s8[16777216]{0:T(1024)(128)(4,1)}), s8[4194304]{0:T(1024)(128)(4,1)S(1)}, s32[]{:S(2)}) async-start(s8[16777216]{0:T(1024)(128)(4,1)} %bitcast.23), calls=%async_computation.6 | async-start | bytes 8388608
  50.0 14.2 %slice-start.2 = ((s8[16777216]{0:T(1024)(128)(4,1)}), s8[4194304]{0:T(1024)(128)(4,1)S(1)}, s32[]{:S(2)}) async-start(s8[16777216]{0:T(1024)(128)(4,1)} %bitcast.23), calls=%async_computation.7 | async-start | bytes 8388608
  50.1 14.2 %slice-start.3 = ((s8[16777216]{0:T(1024)(128)(4,1)}), s8[4194304]{0:T(1024)(128)(4,1)S(1)}, s32[]{:S(2)}) async-start(s8[16777216]{0:T(1024)(128)(4,1)} %bitcast.23), calls=%async_computation.8 | async-start | bytes 8388608
  54.4 34.9 %collective-permute-start.2 = (bf16[256,512]{1,0:T(8,128)(2,1)S(1)}, bf16[256,512]{1,0:T(8,128)(2,1)S(1)}, u32[]{:S(2)}, u32[]{:S(2)}) collective-permute-start(bf16[256,512]{1,0:T(8,128)(2,1)S(1)} %get-tuple-element.12), channel_id=1, source_target_pairs={{0,12},{4,16},{8,20},{12,24},{16,28},{1,13},{5,17},{9,21},{13,25},... | collective-permute-start | bytes 786440 | tf_op jit(solution)/shard_map/ppermute | solution.py:117
  58.9 30.5 %collective-permute-start.1 = (bf16[256,512]{1,0:T(8,128)(2,1)S(1)}, bf16[256,512]{1,0:T(8,128)(2,1)S(1)}, u32[]{:S(2)}, u32[]{:S(2)}) collective-permute-start(bf16[256,512]{1,0:T(8,128)(2,1)S(1)} %get-tuple-element.12), channel_id=1, source_target_pairs={{0,8},{4,12},{8,16},{12,20},{16,24},{20,28},{1,9},{5,13},{9,17},{1... | collective-permute-start | bytes 786440 | tf_op jit(solution)/shard_map/ppermute | solution.py:117
  60.8 28.5 %collective-permute-start = (bf16[256,512]{1,0:T(8,128)(2,1)S(1)}, bf16[256,512]{1,0:T(8,128)(2,1)S(1)}, u32[]{:S(2)}, u32[]{:S(2)}) collective-permute-start(bf16[256,512]{1,0:T(8,128)(2,1)S(1)} %get-tuple-element.12), channel_id=1, source_target_pairs={{0,4},{4,8},{8,12},{12,16},{16,20},{20,24},{24,28},{1,5},{5,9},{9,... | collective-permute-start | bytes 786440 | tf_op jit(solution)/shard_map/ppermute | solution.py:117
  62.7 26.7 %collective-permute-start.3 = (bf16[256,512]{1,0:T(8,128)(2,1)S(1)}, bf16[256,512]{1,0:T(8,128)(2,1)S(1)}, u32[]{:S(2)}, u32[]{:S(2)}) collective-permute-start(bf16[256,512]{1,0:T(8,128)(2,1)S(1)} %get-tuple-element.12), channel_id=1, source_target_pairs={{0,16},{4,20},{8,24},{12,28},{1,17},{5,21},{9,25},{13,29},{2,18},{... | collective-permute-start | bytes 786440 | tf_op jit(solution)/shard_map/ppermute | solution.py:117
  70.9 69.1 %copy-start = (bf16[8192,256]{1,0:T(8,128)(2,1)S(1)}, bf16[8192,256]{1,0:T(8,128)(2,1)}, u32[]{:S(2)}) copy-start(bf16[8192,256]{1,0:T(8,128)(2,1)} %param.10) | copy-start | bytes 12582916
  103.3 19.7 %collective-permute-start.4 = (bf16[256,512]{1,0:T(8,128)(2,1)S(1)}, bf16[256,512]{1,0:T(8,128)(2,1)S(1)}, u32[]{:S(2)}, u32[]{:S(2)}) collective-permute-start(bf16[256,512]{1,0:T(8,128)(2,1)S(1)} %get-tuple-element.8), channel_id=1, source_target_pairs={{4,0},{8,4},{12,8},{16,12},{20,16},{24,20},{28,24},{5,1},{9,5},{13... | collective-permute-start | bytes 786440 | tf_op jit(solution)/shard_map/ppermute | solution.py:117
  110.2 18.4 %collective-permute-start.7 = (bf16[256,512]{1,0:T(8,128)(2,1)S(1)}, bf16[256,512]{1,0:T(8,128)(2,1)S(1)}, u32[]{:S(2)}, u32[]{:S(2)}) collective-permute-start(bf16[256,512]{1,0:T(8,128)(2,1)S(1)} %get-tuple-element.9), channel_id=1, source_target_pairs={{16,0},{20,4},{24,8},{28,12},{17,1},{21,5},{25,9},{29,13},{18,2},{... | collective-permute-start | bytes 786440 | tf_op jit(solution)/shard_map/ppermute | solution.py:117
  111.6 22.7 %collective-permute-start.6 = (bf16[256,512]{1,0:T(8,128)(2,1)S(1)}, bf16[256,512]{1,0:T(8,128)(2,1)S(1)}, u32[]{:S(2)}, u32[]{:S(2)}) collective-permute-start(bf16[256,512]{1,0:T(8,128)(2,1)S(1)} %get-tuple-element.10), channel_id=1, source_target_pairs={{12,0},{16,4},{20,8},{24,12},{28,16},{13,1},{17,5},{21,9},{25,13},... | collective-permute-start | bytes 786440 | tf_op jit(solution)/shard_map/ppermute | solution.py:117
  113.5 26.3 %collective-permute-start.5 = (bf16[256,512]{1,0:T(8,128)(2,1)S(1)}, bf16[256,512]{1,0:T(8,128)(2,1)S(1)}, u32[]{:S(2)}, u32[]{:S(2)}) collective-permute-start(bf16[256,512]{1,0:T(8,128)(2,1)S(1)} %get-tuple-element.11), channel_id=1, source_target_pairs={{8,0},{12,4},{16,8},{20,12},{24,16},{28,20},{9,1},{13,5},{17,9},{2... | collective-permute-start | bytes 786440 | tf_op jit(solution)/shard_map/ppermute | solution.py:117
  140.0 4.5 %copy-start.2 = (bf16[8192,256]{1,0:T(8,128)(2,1)S(1)}, bf16[8192,256]{1,0:T(8,128)(2,1)}, u32[]{:S(2)}) copy-start(bf16[8192,256]{1,0:T(8,128)(2,1)} %param.9) | copy-start | bytes 12582916
Sparse Core Ops, SparseCore 0:
  9.6 35.5 all-gather.1
  164.4 43.6 reduce-scatter.1

commit v2 on v1

--- a/solution.py
+++ b/solution.py
@@ -1,4 +1,3 @@
-import functools
 import math
 
 import jax
@@ -77,38 +76,291 @@
     dk = dot_tn(ds, q)
     dv = dot_tn(wb, go)
     if first:
-        dkv_ref[:, ks] = dk
-        dkv_ref[:, vs] = dv
+        dkv_ref[:, :HD] = dk
+        dkv_ref[:, HD:] = dv
     else:
-        dkv_ref[:, ks] += dk
-        dkv_ref[:, vs] += dv
-
-
-def attn_kernel(heads, start_ref, q_ref, kv_ref, g_ref, att_ref, dq_ref, dkv_ref, bias_ref, sum_ref):
+        dkv_ref[:, :HD] += dk
+        dkv_ref[:, HD:] += dv
+
+
+def back_kernel(
+    start_ref, dest_ref, q_ref, kv_ref, g_ref, wq_hbm, wk_hbm, wv_hbm,
+    got_ref, out_ref,
+    bias, att, dq, sums, send, xrx, zsend, zrx, own, dk, dv, slots, tq,
+    near_tx, near_rx, pre_tx, pre_rx, far_tx, far_rx, wq, wk, wv,
+    wsem, xs, xr, zs, zr, asend, arecv, nts, ntr, pts, ptr, fts, ftr,
+):
     rank = lax.axis_index("ctx")
-    bias_ref[...] = bias_of(start_ref[...], rank, kv_ref.shape[0])
-    for h in range(heads):
-        attend_head(h, q_ref, kv_ref, g_ref, bias_ref, att_ref, dq_ref, sum_ref, h % QPK == 0)
-    dkv_ref[...] = sum_ref[...].astype(BF)
-
-
-def attention(start, q, kv, g):
+    head = lax.axis_index("heads")
+    ranks = lax.axis_size("ctx")
+    nheads = lax.axis_size("heads")
+    chips = nheads // 2
+    core = lax.rem(head, 2)
+    chip = head // 2
+    sib = head + 1 - 2 * core
+    side = lax.rem(rank, 2)
+    pair = rank // 2
+    mate = rank + 1 - 2 * side
+    rows = q_ref.shape[0]
+    qheads = q_ref.shape[1] // HD
+    groups = qheads // QPK
+    back = ranks // 2
+    reach = back // 2
+    chunks = tq.shape[1]
+    width = tq.shape[3]
+    barrier = pltpu.get_barrier_semaphore()
+
+    def to(ctx, h):
+        return dict(device_id=(ctx, h), device_id_type=pl.DeviceIdType.MESH)
+
+    def across(d):
+        return lax.rem(chip + d, chips) * 2 + core
+
+    for o in range(1, ranks):
+        pl.semaphore_signal(barrier, inc=1, **to(lax.rem(rank + o, ranks), head))
+    for d in range(1, chips):
+        pl.semaphore_signal(barrier, inc=1, **to(rank, across(d)))
+    pl.semaphore_signal(barrier, inc=1, **to(rank, sib))
+    loads = [
+        pltpu.make_async_copy(s, t, wsem.at[i])
+        for i, (s, t) in enumerate(((wq_hbm, wq), (wk_hbm, wk), (wv_hbm, wv)))
+    ]
+    for load in loads:
+        load.start()
+    bias[...] = bias_of(start_ref[...], rank, kv_ref.shape[0])
+
+    def xcopy(g, i):
+        return pltpu.make_async_remote_copy(
+            src_ref=send.at[g, 2 * i + 1],
+            dst_ref=xrx.at[g, i + 1],
+            send_sem=xs.at[g, i],
+            recv_sem=xr.at[g, i],
+            **to(mate, head),
+        )
+
+    def zcopy(g, d):
+        return pltpu.make_async_remote_copy(
+            src_ref=zsend.at[g, d - 1],
+            dst_ref=zrx.at[g, d - 1],
+            send_sem=zs.at[g, d - 1],
+            recv_sem=zr.at[g, d - 1],
+            **to(rank - 2 * d, head),
+        )
+
+    def put_dkv(g):
+        send[g] = sums[...].astype(BF).reshape(send.shape[1:])
+        for i in reversed(range(reach)):
+            xcopy(g, i).start()
+
+    def pass_on(g):
+        for i in range(reach):
+            xcopy(g, i).wait()
+        for d in range(reach, -1, -1):
+            both = send[g, 2 * d].astype(F32) + xrx[g, d + 1 - side].astype(F32)
+            if d == 0:
+                own[g] = both
+            else:
+                zsend[g, d - 1] = both.astype(BF)
+
+                @pl.when(pair >= d)
+                def _():
+                    zcopy(g, d).start()
+
+    def collect(g):
+        for d in range(1, reach + 1):
+            @pl.when(pair >= d)
+            def _():
+                zcopy(g, d).wait_send()
+
+            @pl.when(pair + d < ranks // 2)
+            def _():
+                zcopy(g, d).wait_recv()
+                own[g] += zrx[g, d - 1].astype(F32)
+
+        total = own[g].astype(BF)
+        dk[:, g * HD : (g + 1) * HD] = total[:, :HD]
+        dv[:, g * HD : (g + 1) * HD] = total[:, HD:]
+
+    for g in range(groups):
+        xrx[g, 0] = jnp.zeros(xrx.shape[2:], BF)
+        xrx[g, reach + 1] = jnp.zeros(xrx.shape[2:], BF)
+    for g in range(groups):
+        for i in range(QPK):
+            attend_head(g * QPK + i, q_ref, kv_ref, g_ref, bias, att, dq, sums, i == 0)
+            if g > 0 and i == 1:
+                pass_on(g - 1)
+        if g == 0:
+            pl.semaphore_wait(barrier, ranks + chips - 1)
+        put_dkv(g)
+
+    for load in loads:
+        load.wait()
+
+    def piece(t, c):
+        return pl.ds(pl.multiple_of((t * chunks + c) * width, width), width)
+
+    def query_part(t):
+        @pl.loop(0, chunks)
+        def _(c):
+            tq[t, c] = dot_nt(dq[...], wq[piece(t, c), :])
+
+    for d in range(1, chips):
+        query_part(across(d) + 1 - 2 * core)
+    pass_on(groups - 1)
+    nblk = rows // slots.shape[1]
+    block = slots.shape[1]
+
+    def acopy(o):
+        peer = lax.rem(rank + o, ranks)
+        return pltpu.make_async_remote_copy(
+            src_ref=slots.at[o],
+            dst_ref=got_ref.at[rank],
+            send_sem=asend.at[o],
+            recv_sem=arecv.at[o],
+            **to(peer, head),
+        )
+
+    for o in range(ranks):
+        target = lax.rem(rank + o, ranks)
+        value = jnp.zeros(slots.shape[1:], F32)
+        for b in range(nblk):
+            part = slice(b * block, (b + 1) * block)
+            here = (dest_ref[part, :] == target).astype(F32)
+            value = value + att[part, :].astype(F32) * here
+        if o == 0:
+            got_ref[rank] = value.astype(BF)
+        else:
+            slots[o] = value.astype(BF)
+            acopy(o).start()
+    for d in range(1, chips):
+        query_part(across(d))
+    query_part(sib)
+    query_part(head)
+    for g in range(groups):
+        collect(g)
+
+    def term(t, c):
+        at = piece(t, c)
+        return tq[t, c] + dot_nt(dk[...], wk[at, :]) + dot_nt(dv[...], wv[at, :])
+
+    def pre(d, c):
+        return pltpu.make_async_remote_copy(
+            src_ref=pre_tx.at[d - 1, c], dst_ref=pre_rx.at[d - 1, c],
+            send_sem=pts.at[d - 1, c], recv_sem=ptr.at[d - 1, c], **to(rank, sib),
+        )
+
+    def far(d, c):
+        return pltpu.make_async_remote_copy(
+            src_ref=far_tx.at[d - 1, c], dst_ref=far_rx.at[d - 1, c],
+            send_sem=fts.at[d - 1, c], recv_sem=ftr.at[d - 1, c], **to(rank, across(d)),
+        )
+
+    def near(c):
+        return pltpu.make_async_remote_copy(
+            src_ref=near_tx.at[c], dst_ref=near_rx.at[c],
+            send_sem=nts.at[c], recv_sem=ntr.at[c], **to(rank, sib),
+        )
+
+    for d in range(1, chips):
+        @pl.loop(0, chunks)
+        def _(c):
+            pre_tx[d - 1, c] = term(across(d) + 1 - 2 * core, c).astype(BF)
+            pre(d, c).start()
+
+        @pl.loop(0, chunks)
+        def _(c):
+            mine = term(across(d), c)
+            pre(d, c).wait()
+            far_tx[d - 1, c] = (mine + pre_rx[d - 1, c].astype(F32)).astype(BF)
+            far(d, c).start()
+
+    @pl.loop(0, chunks)
+    def _(c):
+        near_tx[c] = term(sib, c).astype(BF)
+        near(c).start()
+
+    @pl.loop(0, chunks)
+    def _(c):
+        tq[head, c] = term(head, c)
+
+    @pl.loop(0, chunks)
+    def _(c):
+        near(c).wait()
+        total = tq[head, c] + near_rx[c].astype(F32)
+        for d in range(1, chips):
+            far(d, c).wait()
+            total = total + far_rx[d - 1, c].astype(F32)
+        out_ref[:, pl.ds(pl.multiple_of(c * width, width), width)] = total.astype(BF)
+
+    for o in range(1, ranks):
+        acopy(o).wait()
+
+
+def backward(start, dest, q, kv, g, w_query, w_key, w_value, block_rows):
+    ranks = lax.axis_size("ctx")
+    nheads = lax.axis_size("heads")
+    chips = nheads // 2
     keys = kv.shape[0]
     rows, width = q.shape
+    feat = w_query.shape[0] // nheads
+    chunks = 4
+    cw = feat // chunks
+    groups = w_key.shape[1] // HD
+    slots = ranks // 2 + 1
+    reach = ranks // 4
     vm = pl.BlockSpec(memory_space=pltpu.VMEM)
+    hbm = pl.BlockSpec(memory_space=pl.ANY)
+    dma = pltpu.SemaphoreType.DMA
     return pl.pallas_call(
-        functools.partial(attn_kernel, width // HD),
+        back_kernel,
         out_shape=(
-            jax.ShapeDtypeStruct((rows, width), BF),
-            jax.ShapeDtypeStruct((rows, width), BF),
-            jax.ShapeDtypeStruct(kv.shape, BF),
+            jax.ShapeDtypeStruct((ranks, block_rows, width), BF),
+            jax.ShapeDtypeStruct((rows, feat), BF),
         ),
-        in_specs=[vm] * 4,
-        out_specs=(vm,) * 3,
-        scratch_shapes=[pltpu.VMEM((rows, keys), F32), pltpu.VMEM(kv.shape, F32)],
-        compiler_params=pltpu.CompilerParams(vmem_limit_bytes=40 * 2**20),
-        name="attention",
-    )(start, q, kv, g)
+        in_specs=[vm] * 5 + [hbm] * 3,
+        out_specs=(vm, vm),
+        scratch_shapes=[
+            pltpu.VMEM((rows, keys), F32),
+            pltpu.VMEM((rows, width), BF),
+            pltpu.VMEM((rows, width), BF),
+            pltpu.VMEM((keys, 2 * HD), F32),
+            pltpu.VMEM((groups, slots, rows, 2 * HD), BF),
+            pltpu.VMEM((groups, reach + 2, rows, 2 * HD), BF),
+            pltpu.VMEM((groups, reach, rows, 2 * HD), BF),
+            pltpu.VMEM((groups, reach, rows, 2 * HD), BF),
+            pltpu.VMEM((groups, rows, 2 * HD), F32),
+            pltpu.VMEM((rows, groups * HD), BF),
+            pltpu.VMEM((rows, groups * HD), BF),
+            pltpu.VMEM((ranks, block_rows, width), BF),
+            pltpu.VMEM((nheads, chunks, rows, cw), F32),
+            pltpu.VMEM((chunks, rows, cw), BF),
+            pltpu.VMEM((chunks, rows, cw), BF),
+            pltpu.VMEM((chips - 1, chunks, rows, cw), BF),
+            pltpu.VMEM((chips - 1, chunks, rows, cw), BF),
+            pltpu.VMEM((chips - 1, chunks, rows, cw), BF),
+            pltpu.VMEM((chips - 1, chunks, rows, cw), BF),
+            pltpu.VMEM(w_query.shape, BF),
+            pltpu.VMEM(w_key.shape, BF),
+            pltpu.VMEM(w_value.shape, BF),
+            dma((3,)),
+            dma((groups, reach)),
+            dma((groups, reach)),
+            dma((groups, reach)),
+            dma((groups, reach)),
+            dma((ranks,)),
+            dma((ranks,)),
+            dma((chunks,)),
+            dma((chunks,)),
+            dma((chips - 1, chunks)),
+            dma((chips - 1, chunks)),
+            dma((chips - 1, chunks)),
+            dma((chips - 1, chunks)),
+        ],
+        compiler_params=pltpu.CompilerParams(
+            vmem_limit_bytes=62 * 2**20, collective_id=1, has_side_effects=True
+        ),
+        name="backward",
+    )(start, dest, q, kv, g, w_query, w_key, w_value)
 
 
 def shift(value, steps):
@@ -148,15 +400,11 @@
     back = ctx_count // 2
     kvs = jnp.concatenate([kv] + [shift(kv, j) for j in range(1, back + 1)], axis=0)
     q = dot_nn(piece, w_query).astype(BF)
-    att, dq, dkvs = attention(start, q, kvs, grad)
-    out = exchange(send_map, att, take_map)
-    total = dkvs[:tok_dev].astype(F32)
-    for j in range(1, back + 1):
-        total = total + shift(dkvs[j * tok_dev : (j + 1) * tok_dev], -j).astype(F32)
-    dkv = total.astype(BF)
-    half = dkv.shape[1] // 2
-    terms = dot_nt(dq, w_query) + dot_nt(dkv[:, :half], w_key) + dot_nt(dkv[:, half:], w_value)
-    input_grad = lax.psum_scatter(terms.astype(BF), "heads", scatter_dimension=1, tiled=True)
+    dest = jnp.repeat(my_dest, block_rows)[:, None]
+    got, input_grad = backward(
+        start, dest, q, kvs, grad, w_query, w_key, w_value, block_rows
+    )
+    out = spread(take_map, got, block_rows).reshape(tok_dev, -1)
     return (out, input_grad)
 
 

time: 217 us -> 173 us (0.80)
  Pallas kernels: 13.8 us -> 69.9 us
  waiting for transfers between devices: 79 us -> 42.4 us
  blocking collectives: 29.1 us -> 0 us
  matrix products: 42 us -> 16.1 us
  starting transfers between devices: 28 us -> 16.1 us
  local copies, waits for them, and re-layouts: 7.16 us -> 11.8 us
    pallas_call x1, Pallas kernels: 13.8 us -> 69.9 us  [backward(): pl.pallas_call(back_kernel, out_shape=(jax.ShapeDtypeStruct((ranks, block...]
    all_to_all x1 -> x0, blocking collectives: 29.1 us -> none  [exchange(): lax.all_to_all(spread(table_out, value, block_rows), 'ctx', split_axis=0,...]
    dot_general x3 -> x0, matrix products: 24.2 us -> none  [dot_nt(): lax.dot_general(a, b, (((1,), (1,)), ((), ())), preferred_element_type=F32)]
    ppermute x8 -> x4, waiting for transfers between devices: 42.8 us -> 19.6 us  [shift(): return lax.ppermute(value, 'ctx', pairs)]
    ppermute x8 -> x4, starting transfers between devices: 21.8 us -> 9.93 us  [shift(): return lax.ppermute(value, 'ctx', pairs)]
    reduce_scatter x1 -> x0, waiting for transfers between devices: 11 us -> none  [per_device(): lax.psum_scatter(terms.astype(BF), 'heads', scatter_dimension=1, tiled=True)]
    unnamed x23 -> x26, local copies, waits for them, and re-layouts: 1.26 us -> 4.61 us
  transfers between devices with their start and end apart: 11 -> 6, of which waited for: 8 -> 3; matrix products, arithmetic and copies ran while one was open for 8% -> 8% of each run, Pallas kernels for 0% -> 0%
where the time goes in v2:
time: 173 us; the launch traced here: 172 us
  Pallas kernels  69.9 us (40%)
  waiting for transfers between devices  42.4 us (25%)
  starting transfers between devices  16.1 us (9%)
  matrix products  16.1 us (9%)
  between operations  14.3 us (8%)
  local copies, waits for them, and re-layouts  11.8 us (7%)
    pallas_call x1, Pallas kernels, backward(): pl.pallas_call(back_kernel, out_shape=(jax.ShapeDtypeStruct((ranks, block...  69.9 us
    all_to_all x1, waiting for transfers between devices, exchange(): lax.all_to_all(spread(table_out, value, block_rows), 'ctx', split_axis=0,...  20.5 us
    ppermute x4, waiting for transfers between devices, shift(): return lax.ppermute(value, 'ctx', pairs)  19.6 us
    dot_general x3, matrix products, dot_nn(): return jnp.dot(a, b, preferred_element_type=F32)  14.5 us
    ppermute x4, starting transfers between devices, shift(): return lax.ppermute(value, 'ctx', pairs)  9.93 us
    all_to_all x1, starting transfers between devices, exchange(): lax.all_to_all(spread(table_out, value, block_rows), 'ctx', split_axis=0,...  6.14 us
    unnamed x26, local copies, waits for them, and re-layouts  4.61 us
  transfers between devices with their start and end apart: 6, of which 3 were waited for; matrix products, arithmetic and copies ran while one was open for 8% of the time, Pallas kernels for 0%

profile of v2, /device:TPU:16, one launch (start us, length us, event | category | flops | bytes accessed | tf_op | source)
XLA Modules:
  0.0 171.9 jit_solution(15137535099453253781)
XLA Ops:
  7.2 0.0 copy-start.4
  7.2 0.0 copy-start.5
  7.2 0.0 all-gather.2.cloned.1.call-start
  7.2 0.7 all-gather.2.cloned.1.call-update
  7.9 1.4 reshape.51
  9.4 0.7 iota_add_fusion.1
  10.0 0.2 convert_reduce_fusion
  10.2 0.1 select_reduce_fusion
  10.3 0.1 and_select_fusion
  10.4 0.6 convolution_convert_fusion
  11.0 1.5 copy.22
  12.6 6.1 %all-to-all-start = ((bf16[8,64,1024]{2,1,0:T(8,128)(2,1)}), bf16[8,64,1024]{2,1,0:T(8,128)(2,1)S(1)}, u32[]{:S(2)}, u32[]{:S(2)}) async-start(bf16[8,64,1024]{2,1,0:T(8,128)(2,1)} %copy.22), calls=%async_computation | async-start | bytes 2097152 | tf_op jit(solution)/shard_map/all_to_all | solution.py:390
  18.7 0.0 copy-done.4
  18.7 0.1 dynamic_slice.7
  18.8 0.0 copy-done.5
  18.8 0.2 reduce-window.8
  19.0 0.1 broadcast_in_dim.44
  19.0 0.8 broadcast_in_dim_reshape.4.dest_ref
  19.8 0.1 select_reduce_fusion.1
  19.9 0.8 copy.23.start_ref
  20.7 20.5 %all-to-all-done = bf16[8,64,1024]{2,1,0:T(8,128)(2,1)S(1)} async-done(((bf16[8,64,1024]{2,1,0:T(8,128)(2,1)}), bf16[8,64,1024]{2,1,0:T(8,128)(2,1)S(1)}, u32[]{:S(2)}, u32[]{:S(2)}) %all-to-all-start) | async-done | bytes 1048608 | tf_op jit(solution)/shard_map/all_to_all | solution.py:390
  41.2 0.6 copy.27
  41.8 0.5 convolution_convert_fusion.2
  42.3 1.2 reshape_reshape.6.g_ref
  43.5 1.7 all-gather.2.cloned.1.call-done
  45.2 0.0 copy-start
  45.2 0.0 slice-start
  45.2 0.0 slice-start.1
  45.2 4.8 %convolution_convert_fusion.4 = bf16[256,256]{1,0:T(8,128)(2,1)S(1)} fusion(bf16[256,8192]{1,0:T(8,128)(2,1)} %all-gather.2.cloned.1.call-done, bf16[8192,256]{1,0:T(8,128)(2,1)} %wv_hbm.1), kind=kOutput, calls=%fused_computation.4 | convolution fusion | flops 1073807360 | bytes 8519680 | tf_op jit(solution)/shard_map/dot_general | solution.py:41
  50.0 0.0 copy-done
  50.0 0.0 slice-start.2
  50.1 0.0 slice-start.3
  50.1 0.0 copy-start.3
  50.1 4.3 %convolution_convert_fusion.5 = bf16[256,256]{1,0:T(8,128)(2,1)S(1)} fusion(bf16[256,8192]{1,0:T(8,128)(2,1)} %all-gather.2.cloned.1.call-done, bf16[8192,256]{1,0:T(8,128)(2,1)S(1)} %copy-done), kind=kOutput, calls=%fused_computation.5 | convolution fusion | flops 1073807360 | bytes 8519680 | tf_op jit(solution)/shard_map/dot_general | solution.py:41
  54.4 4.6 %collective-permute-start.2 = (bf16[256,512]{1,0:T(8,128)(2,1)S(1)}, bf16[256,512]{1,0:T(8,128)(2,1)S(1)}, u32[]{:S(2)}, u32[]{:S(2)}) collective-permute-start(bf16[256,512]{1,0:T(8,128)(2,1)S(1)} %get-tuple-element.6), channel_id=1, source_target_pairs={{0,12},{4,16},{8,20},{12,24},{16,28},{1,13},{5,17},{9,21},{13,25},... | collective-permute-start | bytes 786440 | tf_op jit(solution)/shard_map/ppermute | solution.py:369
  59.0 1.9 %collective-permute-start.1 = (bf16[256,512]{1,0:T(8,128)(2,1)S(1)}, bf16[256,512]{1,0:T(8,128)(2,1)S(1)}, u32[]{:S(2)}, u32[]{:S(2)}) collective-permute-start(bf16[256,512]{1,0:T(8,128)(2,1)S(1)} %get-tuple-element.6), channel_id=1, source_target_pairs={{0,8},{4,12},{8,16},{12,20},{16,24},{20,28},{1,9},{5,13},{9,17},{1... | collective-permute-start | bytes 786440 | tf_op jit(solution)/shard_map/ppermute | solution.py:369
  60.9 2.0 %collective-permute-start = (bf16[256,512]{1,0:T(8,128)(2,1)S(1)}, bf16[256,512]{1,0:T(8,128)(2,1)S(1)}, u32[]{:S(2)}, u32[]{:S(2)}) collective-permute-start(bf16[256,512]{1,0:T(8,128)(2,1)S(1)} %get-tuple-element.6), channel_id=1, source_target_pairs={{0,4},{4,8},{8,12},{12,16},{16,20},{20,24},{24,28},{1,5},{5,9},{9,... | collective-permute-start | bytes 786440 | tf_op jit(solution)/shard_map/ppermute | solution.py:369
  62.9 1.5 collective-permute-start.3
  64.4 0.0 slice-done
  64.4 0.0 slice-done.1
  64.4 0.0 slice-done.2
  64.4 0.0 slice-done.3
  64.4 0.0 copy-done.3
  64.4 5.4 %convolution_convert_fusion.3.q_ref = bf16[256,1024]{1,0:T(8,128)(2,1)} fusion(bf16[256,8192]{1,0:T(8,128)(2,1)S(1)} %copy-done.3, bf16[8192,1024]{1,0:T(8,128)(2,1)S(1)} %bitcast.18), kind=kOutput, calls=%fused_computation.3 | convolution fusion | flops 4295229440 | bytes 21495808 | tf_op jit(solution)/shard_map/dot_general | solution.py:41
  69.8 19.6 %collective-permute-done = bf16[256,512]{1,0:T(8,128)(2,1)S(1)} collective-permute-done((bf16[256,512]{1,0:T(8,128)(2,1)S(1)}, bf16[256,512]{1,0:T(8,128)(2,1)S(1)}, u32[]{:S(2)}, u32[]{:S(2)}) %collective-permute-start) | collective-permute-done | bytes 262176 | tf_op jit(solution)/shard_map/ppermute | solution.py:369
  89.4 0.0 collective-permute-done.1
  89.5 0.0 collective-permute-done.2
  89.5 0.0 collective-permute-done.3
  89.5 0.0 copy-start.1
  89.5 1.1 copy-done.1
  90.6 69.9 %backward.1 = (bf16[8,64,1024]{2,1,0:T(8,128)(2,1)}, bf16[256,2048]{1,0:T(8,128)(2,1)}) custom-call(s32[256,1]{1,0:T(8,128)} %copy.23.start_ref, s32[256,1]{1,0:T(8,128)} %broadcast_in_dim_reshape.4.dest_ref, bf16[256,1024]{1,0:T(8,128)(2,1)} %convolution_convert_fusion.3.q_ref, bf16[1280,512]{1,0:T(8,128)(2,1)} %copy-done.1, ...), custom_call_target="tpu_custom_call" | custom-call | tf_op jit(solution)/shard_map/backward/pallas_call | solution.py:314
  160.5 0.0 copy-start.2
  160.5 1.9 %copy.28 = bf16[1,8,64,1024]{3,1,2,0:T(8,128)(2,1)S(1)} copy(bf16[1,8,64,1024]{3,2,1,0:T(8,128)(2,1)} %bitcast.23) | data formatting | bytes 2097152
  162.4 0.5 convolution_convert_fusion.1
  162.9 1.2 reshape_reshape.7
  164.1 0.0 copy-done.2
  164.1 1.0 copy.34
  (7 shorter events, 0.1 us)
Async XLA Ops:
  7.2 11.5 %copy-start.4 = (s32[32]{0:T(128)S(1)}, s32[32]{0:T(128)}, u32[]{:S(2)}) copy-start(s32[32]{0:T(128)} %param.12) | copy-start | bytes 388
  7.2 11.6 %copy-start.5 = (s32[8]{0:T(128)S(1)}, s32[8]{0:T(128)}, u32[]{:S(2)}) copy-start(s32[8]{0:T(128)} %param.11) | copy-start | bytes 100
  7.2 38.0 %all-gather.2.cloned.1.call-start = ((), (), s32[]{:S(2)}) async-start(), calls=%async_computation.1 | async-start | bytes 5242880 | tf_op jit(solution)/shard_map/all_gather | solution.py:396
  12.6 28.6 %all-to-all-start = ((bf16[8,64,1024]{2,1,0:T(8,128)(2,1)}), bf16[8,64,1024]{2,1,0:T(8,128)(2,1)S(1)}, u32[]{:S(2)}, u32[]{:S(2)}) async-start(bf16[8,64,1024]{2,1,0:T(8,128)(2,1)} %copy.22), calls=%async_computation | async-start | bytes 2097152 | tf_op jit(solution)/shard_map/all_to_all | solution.py:390
  45.2 4.9 %copy-start = (bf16[8192,256]{1,0:T(8,128)(2,1)S(1)}, bf16[8192,256]{1,0:T(8,128)(2,1)}, u32[]{:S(2)}) copy-start(bf16[8192,256]{1,0:T(8,128)(2,1)} %wk_hbm.1) | copy-start | bytes 12582916
  45.2 19.2 %slice-start = ((s8[16777216]{0:T(1024)(128)(4,1)}), s8[4194304]{0:T(1024)(128)(4,1)S(1)}, s32[]{:S(2)}) async-start(s8[16777216]{0:T(1024)(128)(4,1)} %bitcast.17), calls=%async_computation.2 | async-start | bytes 8388608
  45.2 19.2 %slice-start.1 = ((s8[16777216]{0:T(1024)(128)(4,1)}), s8[4194304]{0:T(1024)(128)(4,1)S(1)}, s32[]{:S(2)}) async-start(s8[16777216]{0:T(1024)(128)(4,1)} %bitcast.17), calls=%async_computation.3 | async-start | bytes 8388608
  50.0 14.3 %slice-start.2 = ((s8[16777216]{0:T(1024)(128)(4,1)}), s8[4194304]{0:T(1024)(128)(4,1)S(1)}, s32[]{:S(2)}) async-start(s8[16777216]{0:T(1024)(128)(4,1)} %bitcast.17), calls=%async_computation.4 | async-start | bytes 8388608
  50.1 14.3 %slice-start.3 = ((s8[16777216]{0:T(1024)(128)(4,1)}), s8[4194304]{0:T(1024)(128)(4,1)S(1)}, s32[]{:S(2)}) async-start(s8[16777216]{0:T(1024)(128)(4,1)} %bitcast.17), calls=%async_computation.5 | async-start | bytes 8388608
  50.1 14.3 %copy-start.3 = (bf16[256,8192]{1,0:T(8,128)(2,1)S(1)}, bf16[256,8192]{1,0:T(8,128)(2,1)}, u32[]{:S(2)}) copy-start(bf16[256,8192]{1,0:T(8,128)(2,1)} %all-gather.2.cloned.1.call-done) | copy-start | bytes 12582916
  54.4 35.1 %collective-permute-start.2 = (bf16[256,512]{1,0:T(8,128)(2,1)S(1)}, bf16[256,512]{1,0:T(8,128)(2,1)S(1)}, u32[]{:S(2)}, u32[]{:S(2)}) collective-permute-start(bf16[256,512]{1,0:T(8,128)(2,1)S(1)} %get-tuple-element.6), channel_id=1, source_target_pairs={{0,12},{4,16},{8,20},{12,24},{16,28},{1,13},{5,17},{9,21},{13,25},... | collective-permute-start | bytes 786440 | tf_op jit(solution)/shard_map/ppermute | solution.py:369
  59.0 30.4 %collective-permute-start.1 = (bf16[256,512]{1,0:T(8,128)(2,1)S(1)}, bf16[256,512]{1,0:T(8,128)(2,1)S(1)}, u32[]{:S(2)}, u32[]{:S(2)}) collective-permute-start(bf16[256,512]{1,0:T(8,128)(2,1)S(1)} %get-tuple-element.6), channel_id=1, source_target_pairs={{0,8},{4,12},{8,16},{12,20},{16,24},{20,28},{1,9},{5,13},{9,17},{1... | collective-permute-start | bytes 786440 | tf_op jit(solution)/shard_map/ppermute | solution.py:369
  60.9 28.5 %collective-permute-start = (bf16[256,512]{1,0:T(8,128)(2,1)S(1)}, bf16[256,512]{1,0:T(8,128)(2,1)S(1)}, u32[]{:S(2)}, u32[]{:S(2)}) collective-permute-start(bf16[256,512]{1,0:T(8,128)(2,1)S(1)} %get-tuple-element.6), channel_id=1, source_target_pairs={{0,4},{4,8},{8,12},{12,16},{16,20},{20,24},{24,28},{1,5},{5,9},{9,... | collective-permute-start | bytes 786440 | tf_op jit(solution)/shard_map/ppermute | solution.py:369
  62.9 26.6 %collective-permute-start.3 = (bf16[256,512]{1,0:T(8,128)(2,1)S(1)}, bf16[256,512]{1,0:T(8,128)(2,1)S(1)}, u32[]{:S(2)}, u32[]{:S(2)}) collective-permute-start(bf16[256,512]{1,0:T(8,128)(2,1)S(1)} %get-tuple-element.6), channel_id=1, source_target_pairs={{0,16},{4,20},{8,24},{12,28},{1,17},{5,21},{9,25},{13,29},{2,18},{... | collective-permute-start | bytes 786440 | tf_op jit(solution)/shard_map/ppermute | solution.py:369
  89.5 1.1 copy-start.1
  160.5 3.6 %copy-start.2 = (bf16[256,2048]{1,0:T(8,128)(2,1)S(1)}, bf16[256,2048]{1,0:T(8,128)(2,1)}, u32[]{:S(2)}) copy-start(bf16[256,2048]{1,0:T(8,128)(2,1)} %get-tuple-element.11) | copy-start | bytes 3145732
Sparse Core Ops, SparseCore 0:
  9.6 35.5 all-gather.1

commit v3 on v2

--- a/solution.py
+++ b/solution.py
@@ -363,10 +363,283 @@
     )(start, dest, q, kv, g, w_query, w_key, w_value)
 
 
-def shift(value, steps):
-    count = lax.axis_size("ctx")
-    pairs = [(s, s + steps) for s in range(count) if 0 <= s + steps < count]
-    return lax.ppermute(value, "ctx", pairs)
+def pick(table_ref, wanted, source, block):
+    total = None
+    for b in range(source.shape[0] // block):
+        part = slice(b * block, (b + 1) * block)
+        here = (table_ref[part, :] == wanted).astype(F32)
+        term = source[part, :].astype(F32) * here
+        total = term if total is None else total + term
+    return total.astype(BF)
+
+
+def front_kernel(
+    home_ref, dest_ref, x_ref, grad_ref, wq_hbm, wk_hbm, wv_hbm,
+    q_ref, kv_ref, g_ref,
+    xall, accq, acck, accv, slots, got, wq, wk, wv,
+    wsem, ns, nr, fs, fr, gs, gr, asend, arecv, zs, zr, xs, xr,
+):
+    rank = lax.axis_index("ctx")
+    head = lax.axis_index("heads")
+    ranks = lax.axis_size("ctx")
+    nheads = lax.axis_size("heads")
+    chips = nheads // 2
+    core = lax.rem(head, 2)
+    chip = head // 2
+    turn = 1 - 2 * core
+    sib = head + turn
+    side = lax.rem(rank, 2)
+    pair = rank // 2
+    mate = rank + 1 - 2 * side
+    rows = x_ref.shape[1]
+    block = slots.shape[1]
+    reach = ranks // 4
+    chunks = x_ref.shape[0]
+    width = x_ref.shape[2]
+    feat = chunks * width
+    half = kv_ref.shape[1] // 2
+    barrier = pltpu.get_barrier_semaphore()
+
+    def to(ctx, h):
+        return dict(device_id=(ctx, h), device_id_type=pl.DeviceIdType.MESH)
+
+    def across(d):
+        return lax.rem(chip + d, chips) * 2 + core
+
+    def behind(d):
+        return lax.rem(chip + chips - d, chips) * 2 + core
+
+    for o in range(1, ranks):
+        pl.semaphore_signal(barrier, inc=1, **to(lax.rem(rank + o, ranks), head))
+    for d in range(1, chips):
+        pl.semaphore_signal(barrier, inc=1, **to(rank, across(d)))
+    pl.semaphore_signal(barrier, inc=1, **to(rank, sib))
+
+    order = [head, sib]
+    for d in range(1, chips):
+        order = order + [behind(d), behind(d) + turn]
+
+    def loads(n):
+        at = pl.ds(pl.multiple_of(order[n] * feat, feat), feat)
+        return [
+            pltpu.make_async_copy(s.at[at, :], t.at[at, :], wsem.at[n, i])
+            for i, (s, t) in enumerate(((wq_hbm, wq), (wk_hbm, wk), (wv_hbm, wv)))
+        ]
+
+    for n in range(nheads):
+        for load in loads(n):
+            load.start()
+    pl.semaphore_wait(barrier, ranks + chips - 1)
+
+    def near(c):
+        return pltpu.make_async_remote_copy(
+            src_ref=x_ref.at[c], dst_ref=xall.at[head, c],
+            send_sem=ns.at[c], recv_sem=nr.at[c], **to(rank, sib),
+        )
+
+    def far(d, c):
+        return pltpu.make_async_remote_copy(
+            src_ref=x_ref.at[c], dst_ref=xall.at[head, c],
+            send_sem=fs.at[d - 1, c], recv_sem=fr.at[d - 1, c], **to(rank, across(d)),
+        )
+
+    def give(d, c):
+        return pltpu.make_async_remote_copy(
+            src_ref=xall.at[behind(d), c], dst_ref=xall.at[behind(d), c],
+            send_sem=gs.at[d - 1, c], recv_sem=gr.at[d - 1, c], **to(rank, sib),
+        )
+
+    for d in range(1, chips):
+        for c in range(chunks):
+            far(d, c).start()
+    for c in range(chunks):
+        near(c).start()
+
+    def acopy(o):
+        return pltpu.make_async_remote_copy(
+            src_ref=slots.at[o], dst_ref=got.at[rank],
+            send_sem=asend.at[o], recv_sem=arecv.at[o],
+            **to(lax.rem(rank + o, ranks), head),
+        )
+
+    for o in range(ranks):
+        value = pick(home_ref, lax.rem(rank + o, ranks), grad_ref, block)
+        if o == 0:
+            got[rank] = value
+        else:
+            slots[o] = value
+            acopy(o).start()
+
+    def weights(t, c):
+        return pl.ds(pl.multiple_of(t * feat + c * width, width), width)
+
+    def add_kv(x, t, c):
+        at = weights(t, c)
+        acck[...] += dot_nn(x, wk[at, :])
+        accv[...] += dot_nn(x, wv[at, :])
+
+    def add_q(x, t, c):
+        accq[...] += dot_nn(x, wq[weights(t, c), :])
+
+    accq[...] = jnp.zeros_like(accq)
+    acck[...] = jnp.zeros_like(acck)
+    accv[...] = jnp.zeros_like(accv)
+    for load in loads(0):
+        load.wait()
+
+    @pl.loop(0, chunks)
+    def _(c):
+        add_kv(x_ref[c], head, c)
+        add_q(x_ref[c], head, c)
+
+    for load in loads(1):
+        load.wait()
+
+    @pl.loop(0, chunks)
+    def _(c):
+        near(c).wait()
+        add_kv(xall[sib, c], sib, c)
+        add_q(xall[sib, c], sib, c)
+
+    for n in range(2, nheads):
+        for load in loads(n):
+            load.wait()
+    for d in range(1, chips):
+        one = behind(d)
+        two = one + turn
+
+        @pl.loop(0, chunks)
+        def _(c):
+            far(d, c).wait()
+            give(d, c).start()
+            add_kv(xall[one, c], one, c)
+
+            @pl.when(c > 0)
+            def _():
+                add_q(xall[one, c - 1], one, c - 1)
+                add_q(xall[two, c - 1], two, c - 1)
+
+            give(d, c).wait()
+            add_kv(xall[two, c], two, c)
+
+        if d < chips - 1:
+            add_q(xall[one, chunks - 1], one, chunks - 1)
+            add_q(xall[two, chunks - 1], two, chunks - 1)
+
+    kv_ref[:rows, :half] = acck[...].astype(BF)
+    kv_ref[:rows, half:] = accv[...].astype(BF)
+
+    def slot(j):
+        return pl.ds(pl.multiple_of(j * rows, rows), rows)
+
+    def zcopy(d):
+        return pltpu.make_async_remote_copy(
+            src_ref=kv_ref.at[slot(0), :], dst_ref=kv_ref.at[slot(2 * d), :],
+            send_sem=zs.at[d - 1], recv_sem=zr.at[d - 1], **to(rank + 2 * d, head),
+        )
+
+    def xcopy(i):
+        return pltpu.make_async_remote_copy(
+            src_ref=kv_ref.at[slot(2 * (i + side)), :], dst_ref=kv_ref.at[slot(2 * i + 1), :],
+            send_sem=xs.at[i], recv_sem=xr.at[i], **to(mate, head),
+        )
+
+    for d in range(1, reach + 1):
+        @pl.when(pair + d < ranks // 2)
+        def _():
+            zcopy(d).start()
+
+        @pl.when(pair < d)
+        def _():
+            kv_ref[slot(2 * d), :] = jnp.zeros((rows, 2 * half), BF)
+
+    @pl.when(side == 0)
+    def _():
+        xcopy(0).start()
+
+    one = behind(chips - 1)
+    add_q(xall[one, chunks - 1], one, chunks - 1)
+    add_q(xall[one + turn, chunks - 1], one + turn, chunks - 1)
+    q_ref[...] = accq[...].astype(BF)
+    for o in range(1, ranks):
+        acopy(o).wait()
+    for b in range(rows // block):
+        part = slice(b * block, (b + 1) * block)
+        total = jnp.zeros(slots.shape[1:], F32)
+        for s in range(ranks):
+            total = total + got[s].astype(F32) * (dest_ref[part, :] == s).astype(F32)
+        g_ref[part, :] = total.astype(BF)
+    for d in range(1, reach + 1):
+        @pl.when(pair >= d)
+        def _():
+            zcopy(d).wait_recv()
+
+        if d < reach:
+            @pl.when(side == 0)
+            def _():
+                xcopy(d).start()
+
+        @pl.when(side == 1)
+        def _():
+            xcopy(d - 1).start()
+
+    for i in range(reach):
+        xcopy(i).wait()
+    for d in range(1, reach + 1):
+        @pl.when(pair + d < ranks // 2)
+        def _():
+            zcopy(d).wait_send()
+
+
+def front(home, dest, x, grad, w_query, w_key, w_value, block_rows):
+    ranks = lax.axis_size("ctx")
+    nheads = lax.axis_size("heads")
+    chips = nheads // 2
+    chunks, rows, cw = x.shape
+    width = w_query.shape[1]
+    half = w_key.shape[1]
+    reach = ranks // 4
+    vm = pl.BlockSpec(memory_space=pltpu.VMEM)
+    hbm = pl.BlockSpec(memory_space=pl.ANY)
+    dma = pltpu.SemaphoreType.DMA
+    return pl.pallas_call(
+        front_kernel,
+        out_shape=(
+            jax.ShapeDtypeStruct((rows, width), BF),
+            jax.ShapeDtypeStruct(((ranks // 2 + 1) * rows, 2 * half), BF),
+            jax.ShapeDtypeStruct((rows, width), BF),
+        ),
+        in_specs=[vm] * 4 + [hbm] * 3,
+        out_specs=(vm,) * 3,
+        scratch_shapes=[
+            pltpu.VMEM((nheads, chunks, rows, cw), BF),
+            pltpu.VMEM((rows, width), F32),
+            pltpu.VMEM((rows, half), F32),
+            pltpu.VMEM((rows, half), F32),
+            pltpu.VMEM((ranks, block_rows, width), BF),
+            pltpu.VMEM((ranks, block_rows, width), BF),
+            pltpu.VMEM(w_query.shape, BF),
+            pltpu.VMEM(w_key.shape, BF),
+            pltpu.VMEM(w_value.shape, BF),
+            dma((nheads, 3)),
+            dma((chunks,)),
+            dma((chunks,)),
+            dma((chips - 1, chunks)),
+            dma((chips - 1, chunks)),
+            dma((chips - 1, chunks)),
+            dma((chips - 1, chunks)),
+            dma((ranks,)),
+            dma((ranks,)),
+            dma((reach,)),
+            dma((reach,)),
+            dma((reach,)),
+            dma((reach,)),
+        ],
+        compiler_params=pltpu.CompilerParams(
+            vmem_limit_bytes=60 * 2**20, collective_id=2, has_side_effects=True
+        ),
+        name="front",
+    )(home, dest, x, grad, w_query, w_key, w_value)
 
 
 def per_device(activations, w_query, w_key, w_value, doc_lengths, block_dest, out_grad):
@@ -379,28 +652,17 @@
     ctx_blocks = layout(block_dest)
     slots = jnp.arange(ctx_count, dtype=jnp.int32)
     my_dest = lax.dynamic_slice_in_dim(block_dest, ctx_rank * blocks_here, blocks_here, 0)
-    send_map = (my_dest[None, :] == slots[:, None]).astype(BF)
     mine = lax.dynamic_slice_in_dim(ctx_blocks, ctx_rank * blocks_here, blocks_here, 0)
     take_map = ((mine // blocks_here)[:, None] == slots[None, :]).astype(BF)
     ends = jnp.cumsum(doc_lengths)
     my_pos = ctx_rank * tok_dev + jnp.arange(tok_dev, dtype=jnp.int32)
     start = jnp.max(jnp.where(ends[None, :] <= my_pos[:, None], ends[None, :], 0), axis=1)[:, None]
 
-    def exchange(table_out, value, table_in):
-        sent = lax.all_to_all(
-            spread(table_out, value, block_rows), "ctx", split_axis=0, concat_axis=0, tiled=True
-        )
-        return spread(table_in, sent, block_rows).reshape(tok_dev, -1)
-
-    grad = exchange(take_map.T, out_grad, send_map.T)
-    piece = lax.all_gather(activations, "heads", axis=1, tiled=True)
-    k = dot_nn(piece, w_key).astype(BF)
-    v = dot_nn(piece, w_value).astype(BF)
-    kv = jnp.concatenate([k, v], axis=1)
-    back = ctx_count // 2
-    kvs = jnp.concatenate([kv] + [shift(kv, j) for j in range(1, back + 1)], axis=0)
-    q = dot_nn(piece, w_query).astype(BF)
+    home = jnp.repeat(mine // blocks_here, block_rows)[:, None]
     dest = jnp.repeat(my_dest, block_rows)[:, None]
+    chunks = 4
+    x = activations.reshape(tok_dev, chunks, -1).transpose(1, 0, 2)
+    q, kvs, grad = front(home, dest, x, out_grad, w_query, w_key, w_value, block_rows)
     got, input_grad = backward(
         start, dest, q, kvs, grad, w_query, w_key, w_value, block_rows
     )

time: 173 us -> 138 us (0.80)
  Pallas kernels: 69.9 us -> 124 us
  waiting for transfers between devices: 42.4 us -> 0 us
  starting transfers between devices: 16.1 us -> 0 us
  matrix products: 16.1 us -> 0.49 us
  between operations: 14.3 us -> 0.69 us
    pallas_call x0 -> x1, Pallas kernels: none -> 53.5 us  [front(): pl.pallas_call(front_kernel, out_shape=(jax.ShapeDtypeStruct((rows, width...]
    all_to_all x1 -> x0, waiting for transfers between devices: 20.5 us -> none  [exchange(): lax.all_to_all(spread(table_out, value, block_rows), 'ctx', split_axis=0,...]
    ppermute x4 -> x0, waiting for transfers between devices: 19.6 us -> none  [shift(): return lax.ppermute(value, 'ctx', pairs)]
    dot_general x3 -> x0, matrix products: 14.5 us -> none  [dot_nn(): return jnp.dot(a, b, preferred_element_type=F32)]
    ppermute x4 -> x0, starting transfers between devices: 9.93 us -> none  [shift(): return lax.ppermute(value, 'ctx', pairs)]
    all_to_all x1 -> x0, starting transfers between devices: 6.14 us -> none  [exchange(): lax.all_to_all(spread(table_out, value, block_rows), 'ctx', split_axis=0,...]
    unnamed x26 -> x5, local copies, waits for them, and re-layouts: 4.61 us -> 4.34 us
  transfers between devices with their start and end apart: 6 -> 0, of which waited for: 3 -> 0; matrix products, arithmetic and copies ran while one was open for 8% -> 0% of each run, Pallas kernels for 0% -> 0%
where the time goes in v3:
time: 138 us; the launch traced here: 137 us
  Pallas kernels  124 us (90%)
  local copies, waits for them, and re-layouts  10.1 us (7%)
  other arithmetic  1.96 us (1%)
    pallas_call x1, Pallas kernels, backward(): pl.pallas_call(back_kernel, out_shape=(jax.ShapeDtypeStruct((ranks, block...  70.7 us
    pallas_call x1, Pallas kernels, front(): pl.pallas_call(front_kernel, out_shape=(jax.ShapeDtypeStruct((rows, width...  53.5 us
    unnamed x5, local copies, waits for them, and re-layouts  4.34 us

profile of v3, /device:TPU:16, one launch (start us, length us, event | category | flops | bytes accessed | tf_op | source)
XLA Modules:
  0.0 137.5 jit_solution(16116290502211009191)
XLA Ops:
  0.6 0.8 reduce-window.8
  1.5 0.7 dynamic_slice.7
  2.2 0.7 iota_add_fusion.1
  2.9 0.2 convert_reduce_fusion
  3.0 0.1 select_reduce_fusion
  3.2 0.1 and_select_fusion
  3.2 0.1 select_reduce_fusion.1
  3.3 0.1 broadcast_in_dim.45
  3.4 0.1 broadcast_in_dim.46
  3.5 0.8 broadcast_in_dim_reshape.9.dest_ref
  4.3 0.8 broadcast_in_dim_reshape.8.home_ref
  5.0 0.8 copy.19.start_ref
  5.8 1.5 %copy.15 = bf16[256,2048]{0,1:T(8,128)(2,1)S(1)} copy(bf16[256,2048]{1,0:T(8,128)(2,1)} %param.7) | data formatting | bytes 2097152 | tf_op args[0]
  7.3 1.3 copy.16
  8.7 53.5 %front.1 = (bf16[256,1024]{1,0:T(8,128)(2,1)}, bf16[1280,512]{1,0:T(8,128)(2,1)}, bf16[256,1024]{1,0:T(8,128)(2,1)}) custom-call(s32[256,1]{1,0:T(8,128)} %broadcast_in_dim_reshape.8.home_ref, s32[256,1]{1,0:T(8,128)} %broadcast_in_dim_reshape.9.dest_ref, bf16[4,256,512]{2,1,0:T(8,128)(2,1)} %bitcast.8, bf16[256,1024]{1,0:T(8,128)(2,1)} %grad_ref.1, ...), custom_call_target="tpu_custom_call" | custom-call | tf_op jit(solution)/shard_map/front/pallas_call | solution.py:605
  62.2 70.7 %backward.1 = (bf16[8,64,1024]{2,1,0:T(8,128)(2,1)}, bf16[256,2048]{1,0:T(8,128)(2,1)}) custom-call(s32[256,1]{1,0:T(8,128)} %copy.19.start_ref, s32[256,1]{1,0:T(8,128)} %broadcast_in_dim_reshape.9.dest_ref, bf16[256,1024]{1,0:T(8,128)(2,1)} %get-tuple-element.7.q_ref, bf16[1280,512]{1,0:T(8,128)(2,1)} %get-tuple-element.8.kv_ref, ...), custom_call_target="tpu_custom_call" | custom-call | tf_op jit(solution)/shard_map/backward/pallas_call | solution.py:314
  132.9 0.0 copy-start
  132.9 1.9 %copy.21 = bf16[1,8,64,1024]{3,1,2,0:T(8,128)(2,1)S(1)} copy(bf16[1,8,64,1024]{3,2,1,0:T(8,128)(2,1)} %bitcast.11) | data formatting | bytes 2097152
  134.8 0.5 convolution_convert_fusion
  135.3 1.2 reshape_reshape.3
  136.5 0.0 copy-done
  136.5 1.0 copy.23
  (1 shorter events, 0.0 us)
Async XLA Ops:
  132.9 3.6 %copy-start = (bf16[256,2048]{1,0:T(8,128)(2,1)S(1)}, bf16[256,2048]{1,0:T(8,128)(2,1)}, u32[]{:S(2)}) copy-start(bf16[256,2048]{1,0:T(8,128)(2,1)} %get-tuple-element.15) | copy-start | bytes 3145732

commit v4 on v3

--- a/solution.py
+++ b/solution.py
@@ -14,21 +14,6 @@
 F32 = jnp.float32
 
 
-def layout(block_dest):
-    nblk = block_dest.shape[0]
-    index = jnp.arange(nblk, dtype=jnp.int32)
-    order_key = block_dest * nblk + index
-    ranks = jnp.sum((order_key[None, :] < order_key[:, None]).astype(jnp.int32), axis=1)
-    return jnp.sum(jnp.where(ranks[None, :] == index[:, None], index[None, :], 0), axis=1)
-
-
-def spread(table, array, block_rows):
-    width = array.shape[-1]
-    grouped = array.reshape(table.shape[1], block_rows * width)
-    moved = jnp.dot(table, grouped, preferred_element_type=F32)
-    return moved.astype(BF).reshape(table.shape[0], block_rows, width)
-
-
 def dot_nt(a, b):
     return lax.dot_general(a, b, (((1,), (1,)), ((), ())), preferred_element_type=F32)
 
@@ -39,6 +24,35 @@
 
 def dot_nn(a, b):
     return jnp.dot(a, b, preferred_element_type=F32)
+
+
+def row_starts(len_ref, rank, rows):
+    pos = rank * rows + lax.broadcasted_iota(jnp.int32, (rows, 1), 0)
+    start = jnp.zeros((rows, 1), jnp.int32)
+    end = 0
+    for i in range(len_ref.shape[0]):
+        end = end + len_ref[i]
+        start = jnp.where(pos >= end, end, start)
+    return start
+
+
+def one_if(cond):
+    return jnp.where(cond, 1.0, 0.0)
+
+
+def arrivals(block_ref, rank, ranks):
+    each = block_ref.shape[0] // ranks
+    has = []
+    for t in range(ranks):
+        count = 0
+        for k in range(each):
+            count = count + jnp.where(block_ref[t * each + k] == rank, 1, 0)
+        has.append(count)
+
+    def place(target):
+        return sum(jnp.where(t < target, has[t], 0) for t in range(ranks))
+
+    return has, place
 
 
 def bias_of(start, rank, keys):
@@ -84,9 +98,9 @@
 
 
 def back_kernel(
-    start_ref, dest_ref, q_ref, kv_ref, g_ref, wq_hbm, wk_hbm, wv_hbm,
-    got_ref, out_ref,
-    bias, att, dq, sums, send, xrx, zsend, zrx, own, dk, dv, slots, tq,
+    block_ref, len_ref, q_ref, kv_ref, g_ref, wq_hbm, wk_hbm, wv_hbm,
+    att_ref, out_ref,
+    got_ref, bias, att, dq, sums, send, xrx, zsend, zrx, own, dk, dv, slots, tq,
     near_tx, near_rx, pre_tx, pre_rx, far_tx, far_rx, wq, wk, wv,
     wsem, xs, xr, zs, zr, asend, arecv, nts, ntr, pts, ptr, fts, ftr,
 ):
@@ -127,7 +141,7 @@
     ]
     for load in loads:
         load.start()
-    bias[...] = bias_of(start_ref[...], rank, kv_ref.shape[0])
+    bias[...] = bias_of(row_starts(len_ref, rank, rows), rank, kv_ref.shape[0])
 
     def xcopy(g, i):
         return pltpu.make_async_remote_copy(
@@ -222,20 +236,14 @@
 
     for o in range(ranks):
         target = lax.rem(rank + o, ranks)
-        value = jnp.zeros(slots.shape[1:], F32)
-        for b in range(nblk):
-            part = slice(b * block, (b + 1) * block)
-            here = (dest_ref[part, :] == target).astype(F32)
-            value = value + att[part, :].astype(F32) * here
+        value = pick(att, block, lambda b: one_if(block_ref[rank * nblk + b] == target))
         if o == 0:
-            got_ref[rank] = value.astype(BF)
+            got_ref[rank] = value
         else:
-            slots[o] = value.astype(BF)
+            slots[o] = value
             acopy(o).start()
     for d in range(1, chips):
         query_part(across(d))
-    query_part(sib)
-    query_part(head)
     for g in range(groups):
         collect(g)
 
@@ -274,14 +282,30 @@
             far_tx[d - 1, c] = (mine + pre_rx[d - 1, c].astype(F32)).astype(BF)
             far(d, c).start()
 
+    def direct(t, c):
+        at = piece(t, c)
+        return (
+            dot_nt(dq[...], wq[at, :]) + dot_nt(dk[...], wk[at, :]) + dot_nt(dv[...], wv[at, :])
+        )
+
     @pl.loop(0, chunks)
     def _(c):
-        near_tx[c] = term(sib, c).astype(BF)
+        near_tx[c] = direct(sib, c).astype(BF)
         near(c).start()
 
     @pl.loop(0, chunks)
     def _(c):
-        tq[head, c] = term(head, c)
+        tq[head, c] = direct(head, c)
+
+    for o in range(1, ranks):
+        acopy(o).wait()
+    has, place = arrivals(block_ref, rank, ranks)
+    spots = [place(t) for t in range(ranks)]
+    for b in range(nblk):
+        total = jnp.zeros(slots.shape[1:], F32)
+        for t in range(ranks):
+            total = total + got_ref[t].astype(F32) * one_if((has[t] > 0) & (spots[t] == b))
+        att_ref[b * block : (b + 1) * block, :] = total.astype(BF)
 
     @pl.loop(0, chunks)
     def _(c):
@@ -292,11 +316,8 @@
             total = total + far_rx[d - 1, c].astype(F32)
         out_ref[:, pl.ds(pl.multiple_of(c * width, width), width)] = total.astype(BF)
 
-    for o in range(1, ranks):
-        acopy(o).wait()
-
-
-def backward(start, dest, q, kv, g, w_query, w_key, w_value, block_rows):
+
+def backward(block_dest, doc_lengths, q, kv, g, w_query, w_key, w_value, block_rows):
     ranks = lax.axis_size("ctx")
     nheads = lax.axis_size("heads")
     chips = nheads // 2
@@ -314,12 +335,13 @@
     return pl.pallas_call(
         back_kernel,
         out_shape=(
-            jax.ShapeDtypeStruct((ranks, block_rows, width), BF),
+            jax.ShapeDtypeStruct((rows, width), BF),
             jax.ShapeDtypeStruct((rows, feat), BF),
         ),
-        in_specs=[vm] * 5 + [hbm] * 3,
+        in_specs=[pl.BlockSpec(memory_space=pltpu.SMEM)] * 2 + [vm] * 3 + [hbm] * 3,
         out_specs=(vm, vm),
         scratch_shapes=[
+            pltpu.VMEM((ranks, block_rows, width), BF),
             pltpu.VMEM((rows, keys), F32),
             pltpu.VMEM((rows, width), BF),
             pltpu.VMEM((rows, width), BF),
@@ -360,21 +382,19 @@
             vmem_limit_bytes=62 * 2**20, collective_id=1, has_side_effects=True
         ),
         name="backward",
-    )(start, dest, q, kv, g, w_query, w_key, w_value)
-
-
-def pick(table_ref, wanted, source, block):
+    )(block_dest, doc_lengths, q, kv, g, w_query, w_key, w_value)
+
+
+def pick(source, block, wanted):
     total = None
     for b in range(source.shape[0] // block):
-        part = slice(b * block, (b + 1) * block)
-        here = (table_ref[part, :] == wanted).astype(F32)
-        term = source[part, :].astype(F32) * here
+        term = source[b * block : (b + 1) * block, :].astype(F32) * wanted(b)
         total = term if total is None else total + term
     return total.astype(BF)
 
 
 def front_kernel(
-    home_ref, dest_ref, x_ref, grad_ref, wq_hbm, wk_hbm, wv_hbm,
+    block_ref, x_ref, grad_ref, wq_hbm, wk_hbm, wv_hbm,
     q_ref, kv_ref, g_ref,
     xall, accq, acck, accv, slots, got, wq, wk, wv,
     wsem, ns, nr, fs, fr, gs, gr, asend, arecv, zs, zr, xs, xr,
@@ -391,11 +411,12 @@
     side = lax.rem(rank, 2)
     pair = rank // 2
     mate = rank + 1 - 2 * side
-    rows = x_ref.shape[1]
+    rows = x_ref.shape[0]
     block = slots.shape[1]
+    nblk = rows // block
     reach = ranks // 4
-    chunks = x_ref.shape[0]
-    width = x_ref.shape[2]
+    chunks = xall.shape[1]
+    width = xall.shape[3]
     feat = chunks * width
     half = kv_ref.shape[1] // 2
     barrier = pltpu.get_barrier_semaphore()
@@ -431,15 +452,18 @@
             load.start()
     pl.semaphore_wait(barrier, ranks + chips - 1)
 
+    def cols(c):
+        return pl.ds(pl.multiple_of(c * width, width), width)
+
     def near(c):
         return pltpu.make_async_remote_copy(
-            src_ref=x_ref.at[c], dst_ref=xall.at[head, c],
+            src_ref=x_ref.at[:, cols(c)], dst_ref=xall.at[head, c],
             send_sem=ns.at[c], recv_sem=nr.at[c], **to(rank, sib),
         )
 
     def far(d, c):
         return pltpu.make_async_remote_copy(
-            src_ref=x_ref.at[c], dst_ref=xall.at[head, c],
+            src_ref=x_ref.at[:, cols(c)], dst_ref=xall.at[head, c],
             send_sem=fs.at[d - 1, c], recv_sem=fr.at[d - 1, c], **to(rank, across(d)),
         )
 
@@ -462,8 +486,10 @@
             **to(lax.rem(rank + o, ranks), head),
         )
 
+    has, place = arrivals(block_ref, rank, ranks)
     for o in range(ranks):
-        value = pick(home_ref, lax.rem(rank + o, ranks), grad_ref, block)
+        spot = place(lax.rem(rank + o, ranks))
+        value = pick(grad_ref, block, lambda b: one_if(spot == b))
         if o == 0:
             got[rank] = value
         else:
@@ -489,8 +515,8 @@
 
     @pl.loop(0, chunks)
     def _(c):
-        add_kv(x_ref[c], head, c)
-        add_q(x_ref[c], head, c)
+        add_kv(x_ref[:, cols(c)], head, c)
+        add_q(x_ref[:, cols(c)], head, c)
 
     for load in loads(1):
         load.wait()
@@ -563,12 +589,12 @@
     q_ref[...] = accq[...].astype(BF)
     for o in range(1, ranks):
         acopy(o).wait()
-    for b in range(rows // block):
-        part = slice(b * block, (b + 1) * block)
+    for b in range(nblk):
+        target = block_ref[rank * nblk + b]
         total = jnp.zeros(slots.shape[1:], F32)
         for s in range(ranks):
-            total = total + got[s].astype(F32) * (dest_ref[part, :] == s).astype(F32)
-        g_ref[part, :] = total.astype(BF)
+            total = total + got[s].astype(F32) * one_if(target == s)
+        g_ref[b * block : (b + 1) * block, :] = total.astype(BF)
     for d in range(1, reach + 1):
         @pl.when(pair >= d)
         def _():
@@ -591,11 +617,13 @@
             zcopy(d).wait_send()
 
 
-def front(home, dest, x, grad, w_query, w_key, w_value, block_rows):
+def front(block_dest, x, grad, w_query, w_key, w_value, block_rows):
     ranks = lax.axis_size("ctx")
     nheads = lax.axis_size("heads")
     chips = nheads // 2
-    chunks, rows, cw = x.shape
+    chunks = 4
+    rows = x.shape[0]
+    cw = x.shape[1] // chunks
     width = w_query.shape[1]
     half = w_key.shape[1]
     reach = ranks // 4
@@ -609,7 +637,7 @@
             jax.ShapeDtypeStruct(((ranks // 2 + 1) * rows, 2 * half), BF),
             jax.ShapeDtypeStruct((rows, width), BF),
         ),
-        in_specs=[vm] * 4 + [hbm] * 3,
+        in_specs=[pl.BlockSpec(memory_space=pltpu.SMEM)] + [vm] * 2 + [hbm] * 3,
         out_specs=(vm,) * 3,
         scratch_shapes=[
             pltpu.VMEM((nheads, chunks, rows, cw), BF),
@@ -639,35 +667,14 @@
             vmem_limit_bytes=60 * 2**20, collective_id=2, has_side_effects=True
         ),
         name="front",
-    )(home, dest, x, grad, w_query, w_key, w_value)
+    )(block_dest, x, grad, w_query, w_key, w_value)
 
 
 def per_device(activations, w_query, w_key, w_value, doc_lengths, block_dest, out_grad):
-    ctx_count = lax.axis_size("ctx")
-    ctx_rank = lax.axis_index("ctx")
-    tok_dev = activations.shape[0]
-    nblk = block_dest.shape[0]
-    block_rows = tok_dev * ctx_count // nblk
-    blocks_here = tok_dev // block_rows
-    ctx_blocks = layout(block_dest)
-    slots = jnp.arange(ctx_count, dtype=jnp.int32)
-    my_dest = lax.dynamic_slice_in_dim(block_dest, ctx_rank * blocks_here, blocks_here, 0)
-    mine = lax.dynamic_slice_in_dim(ctx_blocks, ctx_rank * blocks_here, blocks_here, 0)
-    take_map = ((mine // blocks_here)[:, None] == slots[None, :]).astype(BF)
-    ends = jnp.cumsum(doc_lengths)
-    my_pos = ctx_rank * tok_dev + jnp.arange(tok_dev, dtype=jnp.int32)
-    start = jnp.max(jnp.where(ends[None, :] <= my_pos[:, None], ends[None, :], 0), axis=1)[:, None]
-
-    home = jnp.repeat(mine // blocks_here, block_rows)[:, None]
-    dest = jnp.repeat(my_dest, block_rows)[:, None]
-    chunks = 4
-    x = activations.reshape(tok_dev, chunks, -1).transpose(1, 0, 2)
-    q, kvs, grad = front(home, dest, x, out_grad, w_query, w_key, w_value, block_rows)
-    got, input_grad = backward(
-        start, dest, q, kvs, grad, w_query, w_key, w_value, block_rows
-    )
-    out = spread(take_map, got, block_rows).reshape(tok_dev, -1)
-    return (out, input_grad)
+    weights = (w_query, w_key, w_value)
+    block_rows = activations.shape[0] * lax.axis_size("ctx") // block_dest.shape[0]
+    q, kv, grad = front(block_dest, activations, out_grad, *weights, block_rows)
+    return backward(block_dest, doc_lengths, q, kv, grad, *weights, block_rows)
 
 
 def solution(mesh):

time: 138 us -> 129 us (0.935)
  local copies, waits for them, and re-layouts: 10.1 us -> 4.17 us
  other arithmetic: 1.96 us -> 0 us
    another operation x3 -> x0, local copies, waits for them, and re-layouts: 2.8 us -> none  [the longest x1 1.22 us: per_device(): out = spread(take_map, got, block_rows).reshape(tok_dev, -1)]
    unnamed x5 -> x2, local copies, waits for them, and re-layouts: 4.34 us -> 4.17 us
where the time goes in v4:
time: 129 us
  Pallas kernels  124 us (96%)
  local copies, waits for them, and re-layouts  4.17 us (3%)
    pallas_call x1, Pallas kernels, backward(): pl.pallas_call(back_kernel, out_shape=(jax.ShapeDtypeStruct((rows, width)...  70.7 us
    pallas_call x1, Pallas kernels, front(): pl.pallas_call(front_kernel, out_shape=(jax.ShapeDtypeStruct((rows, width...  53.4 us
    unnamed x2, local copies, waits for them, and re-layouts  4.17 us

profile of v4, /device:TPU:16, one launch (start us, length us, event | category | flops | bytes accessed | tf_op | source)
XLA Modules:
  0.0 129.0 jit_solution(8615000182657994639)
XLA Ops:
  0.6 53.4 %front.1 = (bf16[256,1024]{1,0:T(8,128)(2,1)}, bf16[1280,512]{1,0:T(8,128)(2,1)}, bf16[256,1024]{1,0:T(8,128)(2,1)}) custom-call(s32[32]{0:T(128)} %block_ref.3, bf16[256,2048]{1,0:T(8,128)(2,1)} %x_ref.1, bf16[256,1024]{1,0:T(8,128)(2,1)} %grad_ref.1, bf16[8192,1024]{1,0:T(8,128)(2,1)} %wq_hbm.3, bf16[8192,256]{1,0:T(8,128)(2,1)} %wk_hbm.3, ...), custom_call_target="tpu_custom_call" | custom-call | tf_op jit(solution)/shard_map/front/pallas_call | solution.py:633
  54.1 70.7 %backward.1 = (bf16[256,1024]{1,0:T(8,128)(2,1)}, bf16[256,2048]{1,0:T(8,128)(2,1)}) custom-call(s32[32]{0:T(128)} %block_ref.3, s32[8]{0:T(128)} %len_ref.1, bf16[256,1024]{1,0:T(8,128)(2,1)} %get-tuple-element.5.q_ref, bf16[1280,512]{1,0:T(8,128)(2,1)} %get-tuple-element.6.kv_ref, bf16[256,1024]{1,0:T(8,128)(2,1)} %get-tuple-element.7.g_ref, ...), custom_call_target="tpu_custom_call" | custom-call | tf_op jit(solution)/shard_map/backward/pallas_call | solution.py:335
  124.8 1.9 %copy.11 = bf16[256,1024]{1,0:T(8,128)(2,1)} copy(bf16[256,1024]{1,0:T(8,128)(2,1)} %get-tuple-element.10) | data formatting | bytes 1048576
  126.7 2.3 %copy.12 = bf16[256,2048]{1,0:T(8,128)(2,1)} copy(bf16[256,2048]{1,0:T(8,128)(2,1)} %get-tuple-element.11) | data formatting | bytes 2097152

commit v5 on v4

--- a/solution.py
+++ b/solution.py
@@ -241,11 +241,12 @@
             got_ref[rank] = value
         else:
             slots[o] = value
-            acopy(o).start()
     for d in range(1, chips):
         query_part(across(d))
     for g in range(groups):
         collect(g)
+    for o in range(1, ranks):
+        acopy(o).start()
 
     def term(t, c):
         at = piece(t, c)

time: 129 us -> 124 us (0.961)
  Pallas kernels: 124 us -> 119 us
    pallas_call x1, Pallas kernels: 70.7 us -> 65.8 us  [backward(): pl.pallas_call(back_kernel, out_shape=(jax.ShapeDtypeStruct((rows, width)...]
where the time goes in v5:
time: 124 us
  Pallas kernels  119 us (96%)
  local copies, waits for them, and re-layouts  4.17 us (3%)
    pallas_call x1, Pallas kernels, backward(): pl.pallas_call(back_kernel, out_shape=(jax.ShapeDtypeStruct((rows, width)...  65.8 us
    pallas_call x1, Pallas kernels, front(): pl.pallas_call(front_kernel, out_shape=(jax.ShapeDtypeStruct((rows, width...  53.4 us
    unnamed x2, local copies, waits for them, and re-layouts  4.17 us

profile of v5, /device:TPU:16, one launch (start us, length us, event | category | flops | bytes accessed | tf_op | source)
XLA Modules:
  0.0 124.1 jit_solution(10416669673188048760)
XLA Ops:
  0.6 53.4 %front.1 = (bf16[256,1024]{1,0:T(8,128)(2,1)}, bf16[1280,512]{1,0:T(8,128)(2,1)}, bf16[256,1024]{1,0:T(8,128)(2,1)}) custom-call(s32[32]{0:T(128)} %block_ref.3, bf16[256,2048]{1,0:T(8,128)(2,1)} %x_ref.1, bf16[256,1024]{1,0:T(8,128)(2,1)} %grad_ref.1, bf16[8192,1024]{1,0:T(8,128)(2,1)} %wq_hbm.3, bf16[8192,256]{1,0:T(8,128)(2,1)} %wk_hbm.3, ...), custom_call_target="tpu_custom_call" | custom-call | tf_op jit(solution)/shard_map/front/pallas_call | solution.py:634
  54.1 65.8 %backward.1 = (bf16[256,1024]{1,0:T(8,128)(2,1)}, bf16[256,2048]{1,0:T(8,128)(2,1)}) custom-call(s32[32]{0:T(128)} %block_ref.3, s32[8]{0:T(128)} %len_ref.1, bf16[256,1024]{1,0:T(8,128)(2,1)} %get-tuple-element.5.q_ref, bf16[1280,512]{1,0:T(8,128)(2,1)} %get-tuple-element.6.kv_ref, bf16[256,1024]{1,0:T(8,128)(2,1)} %get-tuple-element.7.g_ref, ...), custom_call_target="tpu_custom_call" | custom-call | tf_op jit(solution)/shard_map/backward/pallas_call | solution.py:336
  119.9 1.9 %copy.11 = bf16[256,1024]{1,0:T(8,128)(2,1)} copy(bf16[256,1024]{1,0:T(8,128)(2,1)} %get-tuple-element.10) | data formatting | bytes 1048576
  121.8 2.3 %copy.12 = bf16[256,2048]{1,0:T(8,128)(2,1)} copy(bf16[256,2048]{1,0:T(8,128)(2,1)} %get-tuple-element.11) | data formatting | bytes 2097152
